TPU v7x, 32 devices: a whole 2x2x4 slice. The times are simulated.
32 devices in a mesh: dp: 8 (over z, core), expert: 4 (over y, x).
Axes of the slice: x: 2, y: 2, z: 4, core: 2. Of those that a mesh axis runs over, the one named last changes fastest.
Arguments:
- images: bfloat16 [128, 196, 768], P(('dp', 'expert')), may hold values from -6 to 6
- cotangent: bfloat16 [128, 196, 768], P(('dp', 'expert')), may hold values from -6 to 6
- gains: float32 [2, 768], replicated, may hold values from 0.5 to 1.5
- qkv_weight: bfloat16 [768, 2304], replicated, may hold values from -0.21875 to 0.21875
- out_weight: bfloat16 [768, 768], replicated, may hold values from -0.875 to 0.875
- router_weight: bfloat16 [768, 4], replicated, may hold values from -0.4375 to 0.4375
- up_weight: bfloat16 [4, 768, 3072], P('expert'), may hold values from -0.21875 to 0.21875
- down_weight: bfloat16 [4, 3072, 768], P('expert'), may hold values from -0.875 to 0.875
- choices: int32 [128, 196, 2], P(('dp', 'expert')), may hold values from 0 to 3, as said below
- slots: int32 [128, 196, 2], P(('dp', 'expert')), may hold values from -1 to 411, as said below
- owner_shared: int32 [16], replicated, may hold values from 0 to 15, as said below
- owner_expert: int32 [4, 32], P('expert'), may hold values from 0 to 31, as said below
- shared_m: float32 [16, 384, 384], P('dp')
- shared_v: float32 [16, 384, 384], P('dp'), as said below
- shared_left: float32 [16, 384, 384], P('dp'), may hold values from -1 to 1, as said below
- shared_right: float32 [16, 384, 384], P('dp'), may hold values from -1 to 1, as said below
- expert_m: float32 [4, 32, 384, 384], P('expert', 'dp')
- expert_v: float32 [4, 32, 384, 384], P('expert', 'dp'), as said below
- expert_left: float32 [4, 32, 384, 384], P('expert', 'dp'), may hold values from -1 to 1, as said below
- expert_right: float32 [4, 32, 384, 384], P('expert', 'dp'), may hold values from -1 to 1, as said below
- router_m: float32 [768, 4], replicated
- router_v: float32 [768, 4], replicated, as said below
- gains_m: float32 [2, 768], replicated
- gains_v: float32 [2, 768], replicated, as said below
Outputs:
- out: bfloat16 [128, 196, 768], P(('dp', 'expert'))
- grad_input: float32 [128, 196, 768], P(('dp', 'expert'))
- shared_m_new: float32 [16, 384, 384], P('dp')
- shared_v_new: float32 [16, 384, 384], P('dp')
- shared_w_new: float32 [16, 384, 384], P('dp')
- expert_m_new: float32 [4, 32, 384, 384], P('expert', 'dp')
- expert_v_new: float32 [4, 32, 384, 384], P('expert', 'dp')
- expert_w_new: float32 [4, 32, 384, 384], P('expert', 'dp')
- router_m_new: float32 [768, 4], replicated
- router_v_new: float32 [768, 4], replicated
- router_w_new: float32 [768, 4], replicated
- gains_m_new: float32 [2, 768], replicated
- gains_v_new: float32 [2, 768], replicated
- gains_w_new: float32 [2, 768], replicated
- qkv_copy: bfloat16 [768, 2304], replicated
- out_copy: bfloat16 [768, 768], replicated
- up_copy: bfloat16 [4, 768, 3072], P('expert')
- down_copy: bfloat16 [4, 3072, 768], P('expert')
Inputs may be any that keep to these rules, and one draw needn't show every extreme that they name: `choices`: the two experts of a patch differ. `slots`: -1 marks a dropped pair. Within the pairs of one device's patches (aligned blocks of 784 patches) the places of one expert are 0, 1, 2, ... without gaps or repeats, given first to all first choices, then to second choices; a pair is dropped only when 412 places of its expert are taken. `owner_shared`: A permutation of the tiles. `owner_expert`: each row is a permutation of the tiles. `shared_left`: orthogonal matrices. `shared_right`: orthogonal matrices. `expert_left`: orthogonal matrices. `expert_right`: orthogonal matrices. `shared_v`: Positive. `expert_v`: Positive. `router_v`: Positive. `gains_v`: Positive.
All inputs are finite; a program needn't handle non-finite values.
Results may differ from a plain program's by a relative error of at most 0.023.
Values may be sent and summed in bfloat16 or wider, within the bound.
No kernel may reach another device: no remote copies, remote signals or barrier semaphores. Data moves between devices by JAX's collectives and lax.ppermute only.
A program may use at most 256 MiB of HBM per device.

v0:
```python
import jax
import jax.numpy as jnp
from jax import lax
from jax.sharding import PartitionSpec as P

HEADS = 12
HEAD_DIM = 64
TILE = 384


precise = lax.Precision.HIGHEST
norm_eps = 1e-06
adam_beta = 0.5
adam_eps = 1e-08
adam_step = 5
rate_scale = 0.3


def norm_stats(values):
    center = values - jnp.mean(values, axis=-1, keepdims=True)
    inv_std = lax.rsqrt(jnp.mean(center * center, axis=-1, keepdims=True) + norm_eps)
    return (center * inv_std, inv_std)


def norm_back(grad_normed, unit_rows, inv_std, gain_row):
    grad_hat = grad_normed * gain_row
    gain_grad = jnp.sum(grad_normed * unit_rows, axis=0)
    mean_one = jnp.mean(grad_hat, axis=-1, keepdims=True)
    mean_two = jnp.mean(grad_hat * unit_rows, axis=-1, keepdims=True)
    return (inv_std * (grad_hat - mean_one - unit_rows * mean_two), gain_grad)


def exact_gelu(values):
    return jax.nn.gelu(values, approximate=False)


def to_tiles(matrix):
    row_count = matrix.shape[-2]
    col_count = matrix.shape[-1]
    leading = matrix.shape[:-2]
    blocked = matrix.reshape(leading + (row_count // TILE, TILE, col_count // TILE, TILE))
    return jnp.swapaxes(blocked, -3, -2).reshape(leading + (-1, TILE, TILE))


def from_tiles(tiles, row_count, col_count):
    leading = tiles.shape[:-3]
    blocked = tiles.reshape(leading + (row_count // TILE, col_count // TILE, TILE, TILE))
    return jnp.swapaxes(blocked, -3, -2).reshape(leading + (row_count, col_count))


def rotated_adam(grad_tiles, weight_tiles, first_moment, second_moment, left_basis, right_basis):
    turned = jnp.einsum("...ji,...jk->...ik", left_basis, grad_tiles, precision=precise)
    turned = jnp.einsum("...ik,...kl->...il", turned, right_basis, precision=precise)
    first_new = adam_beta * first_moment + (1.0 - adam_beta) * turned
    second_new = adam_beta * second_moment + (1.0 - adam_beta) * turned * turned
    correction = 1.0 - adam_beta**adam_step
    direction = first_new / correction / (jnp.sqrt(second_new / correction) + adam_eps)
    back_turn = jnp.einsum("...ij,...jk->...ik", left_basis, direction, precision=precise)
    back_turn = jnp.einsum("...ik,...lk->...il", back_turn, right_basis, precision=precise)
    step_rate = rate_scale * jnp.sqrt(
        jnp.mean(weight_tiles * weight_tiles, axis=(-2, -1), keepdims=True)
    )
    return (first_new, second_new, weight_tiles - step_rate * back_turn)


def plain_adam(grad_values, weight_values, first_moment, second_moment, axes):
    first_new = adam_beta * first_moment + (1.0 - adam_beta) * grad_values
    second_new = adam_beta * second_moment + (1.0 - adam_beta) * grad_values * grad_values
    correction = 1.0 - adam_beta**adam_step
    direction = first_new / correction / (jnp.sqrt(second_new / correction) + adam_eps)
    step_rate = rate_scale * jnp.sqrt(
        jnp.mean(weight_values * weight_values, axis=axes, keepdims=True)
    )
    return (first_new, second_new, weight_values - step_rate * direction)


def shards(
    images,
    cotangent,
    gains,
    qkv_weight,
    out_weight,
    router_weight,
    up_weight,
    down_weight,
    choices,
    slots,
    owner_shared,
    owner_expert,
    shared_m,
    shared_v,
    shared_left,
    shared_right,
    expert_m,
    expert_v,
    expert_left,
    expert_right,
    router_m,
    router_v,
    gains_m,
    gains_v,
):
    image_count, patch_count, model_width = images.shape
    token_count = image_count * patch_count
    group_size = lax.axis_size("expert")
    dp_size = lax.axis_size("dp")
    local_experts = up_weight.shape[0]
    hidden_width = up_weight.shape[2]
    expert_total = router_weight.shape[1]
    capacity = (42 * token_count + 20 * expert_total - 1) // (20 * expert_total)
    place_count = expert_total * capacity
    score_scale = HEAD_DIM ** (-0.5)
    tokens = images.reshape(token_count, model_width).astype(jnp.float32)
    unit_one, inv_one = norm_stats(tokens)
    normed = (unit_one * gains[0]).astype(jnp.bfloat16)
    qkv_rows = jnp.dot(normed, qkv_weight, preferred_element_type=jnp.float32).astype(jnp.bfloat16)
    head_major = jnp.transpose(
        qkv_rows.reshape(image_count, patch_count, 3, HEADS, HEAD_DIM), (2, 0, 3, 1, 4)
    )
    queries = head_major[0]
    key_rows = head_major[1]
    value_rows = head_major[2]
    gating_logit_matrix = (
        jnp.einsum("ihqd,ihkd->ihqk", queries, key_rows, preferred_element_type=jnp.float32)
        * score_scale
    )
    row_peak = jnp.max(gating_logit_matrix, axis=-1, keepdims=True)
    expo = jnp.exp(gating_logit_matrix - row_peak)
    row_total = jnp.sum(expo, axis=-1, keepdims=True)
    attn_weights = expo / row_total
    log_total = row_peak + jnp.log(row_total)
    mixed_heads = jnp.einsum(
        "ihqk,ihkd->ihqd",
        attn_weights.astype(jnp.bfloat16),
        value_rows,
        preferred_element_type=jnp.float32,
    ).astype(jnp.bfloat16)
    mixed_rows = jnp.transpose(mixed_heads, (0, 2, 1, 3)).reshape(token_count, model_width)
    hidden = tokens + jnp.dot(mixed_rows, out_weight, preferred_element_type=jnp.float32)
    unit_two, inv_two = norm_stats(hidden)
    routed = (unit_two * gains[1]).astype(jnp.bfloat16)
    logits = jnp.dot(routed, router_weight, preferred_element_type=jnp.float32)
    router_probs = jax.nn.softmax(logits, axis=-1)
    choice_rows = choices.reshape(token_count, 2)
    slot_rows = slots.reshape(token_count, 2)
    kept_pairs = slot_rows >= 0
    flat_place = jnp.where(kept_pairs, choice_rows * capacity + slot_rows, place_count)
    pair_table = (
        jnp.full((place_count + 1,), 2 * token_count, jnp.int32)
        .at[flat_place.reshape(-1)]
        .set(jnp.arange(2 * token_count, dtype=jnp.int32))[:place_count]
    )
    routed_pad = jnp.concatenate([routed, jnp.zeros((1, model_width), jnp.bfloat16)], axis=0)
    outgoing = routed_pad[pair_table // 2].reshape(expert_total, capacity, model_width)
    gate_values = jnp.where(kept_pairs, jnp.take_along_axis(router_probs, choice_rows, axis=1), 0.0)
    arriving = lax.all_to_all(outgoing, "expert", split_axis=0, concat_axis=0, tiled=True)
    item_count = arriving.shape[1]
    grouped = arriving.reshape(group_size, local_experts, item_count, model_width)
    pre_act = jnp.einsum("sjcd,jdf->sjcf", grouped, up_weight, preferred_element_type=jnp.float32)
    activated = exact_gelu(pre_act).astype(jnp.bfloat16)
    produced = jnp.einsum(
        "sjcf,jfd->sjcd", activated, down_weight, preferred_element_type=jnp.float32
    ).astype(jnp.bfloat16)
    returned = lax.all_to_all(
        produced.reshape(group_size * local_experts, item_count, model_width),
        "expert",
        split_axis=0,
        concat_axis=0,
        tiled=True,
    )
    back_pad = jnp.concatenate(
        [returned.reshape(place_count, model_width), jnp.zeros((1, model_width), jnp.bfloat16)],
        axis=0,
    )
    pair_out = back_pad[flat_place].astype(jnp.float32)
    mixture = jnp.sum(gate_values[:, :, None] * pair_out, axis=1)
    out = (hidden + mixture).astype(jnp.bfloat16).reshape(images.shape)
    upstream = cotangent.reshape(token_count, model_width).astype(jnp.float32)
    gate_grad = jnp.where(kept_pairs, jnp.sum(upstream[:, None, :] * pair_out, axis=-1), 0.0)
    onehot = (
        choice_rows[:, :, None] == jnp.arange(expert_total, dtype=jnp.int32)[None, None, :]
    ).astype(jnp.float32)
    prob_grad = jnp.sum(onehot * gate_grad[:, :, None], axis=1)
    logit_grad = router_probs * (
        prob_grad - jnp.sum(router_probs * prob_grad, axis=-1, keepdims=True)
    )
    logit_low = logit_grad.astype(jnp.bfloat16)
    router_grad = jnp.dot(routed.T, logit_low, preferred_element_type=jnp.float32)
    routed_grad = jnp.dot(logit_low, router_weight.T, preferred_element_type=jnp.float32)
    pair_grad = (
        (gate_values[:, :, None] * upstream[:, None, :])
        .astype(jnp.bfloat16)
        .reshape(2 * token_count, model_width)
    )
    pair_pad = jnp.concatenate([pair_grad, jnp.zeros((1, model_width), jnp.bfloat16)], axis=0)
    outgoing_grad = pair_pad[pair_table].reshape(expert_total, capacity, model_width)
    arriving_grad = lax.all_to_all(outgoing_grad, "expert", split_axis=0, concat_axis=0, tiled=True)
    grouped_in = arriving.reshape(group_size, local_experts, capacity, model_width)
    grouped_grad = arriving_grad.reshape(group_size, local_experts, capacity, model_width)
    pre_act = pre_act.reshape(group_size * local_experts, item_count, hidden_width).reshape(
        group_size, local_experts, capacity, hidden_width
    )
    activated, gelu_back = jax.vjp(exact_gelu, pre_act)
    act_low = activated.astype(jnp.bfloat16)
    act_grad = jnp.einsum(
        "sjcd,jfd->sjcf", grouped_grad, down_weight, preferred_element_type=jnp.float32
    )
    pre_grad = gelu_back(act_grad)[0].astype(jnp.bfloat16)
    down_grad = jnp.einsum(
        "sjcf,sjcd->jfd", act_low, grouped_grad, preferred_element_type=jnp.float32
    )
    up_grad = jnp.einsum("sjcd,sjcf->jdf", grouped_in, pre_grad, preferred_element_type=jnp.float32)
    input_rows_grad = jnp.einsum(
        "sjcf,jdf->sjcd", pre_grad, up_weight, preferred_element_type=jnp.float32
    ).astype(jnp.bfloat16)
    returned_grad = lax.all_to_all(
        input_rows_grad.reshape(group_size * local_experts, capacity, model_width),
        "expert",
        split_axis=0,
        concat_axis=0,
        tiled=True,
    )
    grad_pad = jnp.concatenate(
        [
            returned_grad.reshape(place_count, model_width),
            jnp.zeros((1, model_width), jnp.bfloat16),
        ],
        axis=0,
    )
    routed_grad = routed_grad + jnp.sum(grad_pad[flat_place].astype(jnp.float32), axis=1)
    norm_grad_two, gain_grad_two = norm_back(routed_grad, unit_two, inv_two, gains[1])
    hidden_grad = upstream + norm_grad_two
    branch_low = hidden_grad.astype(jnp.bfloat16)
    out_grad = jnp.dot(mixed_rows.T, branch_low, preferred_element_type=jnp.float32)
    mixed_grad_rows = jnp.dot(branch_low, out_weight.T, preferred_element_type=jnp.float32).astype(
        jnp.bfloat16
    )
    mixed_grad = jnp.transpose(
        mixed_grad_rows.reshape(image_count, patch_count, HEADS, HEAD_DIM), (0, 2, 1, 3)
    )
    scores_again = (
        jnp.einsum("ihqd,ihkd->ihqk", queries, key_rows, preferred_element_type=jnp.float32)
        * score_scale
    )
    weights_again = jnp.exp(scores_again - log_total)
    weight_grad = jnp.einsum(
        "ihqd,ihkd->ihqk", mixed_grad, value_rows, preferred_element_type=jnp.float32
    )
    inner = jnp.sum(weights_again * weight_grad, axis=-1, keepdims=True)
    score_grad = (weights_again * (weight_grad - inner)).astype(jnp.bfloat16)
    query_grad = (
        jnp.einsum("ihqk,ihkd->ihqd", score_grad, key_rows, preferred_element_type=jnp.float32)
        * score_scale
    )
    key_grad = (
        jnp.einsum("ihqk,ihqd->ihkd", score_grad, queries, preferred_element_type=jnp.float32)
        * score_scale
    )
    value_grad = jnp.einsum(
        "ihqk,ihqd->ihkd",
        weights_again.astype(jnp.bfloat16),
        mixed_grad,
        preferred_element_type=jnp.float32,
    )
    head_grads = jnp.stack([query_grad, key_grad, value_grad], axis=0).astype(jnp.bfloat16)
    qkv_grad = jnp.transpose(head_grads, (1, 3, 0, 2, 4)).reshape(token_count, 3 * model_width)
    qkv_weight_grad = jnp.dot(normed.T, qkv_grad, preferred_element_type=jnp.float32)
    normed_grad = jnp.dot(qkv_grad, qkv_weight.T, preferred_element_type=jnp.float32)
    norm_grad_one, gain_grad_one = norm_back(normed_grad, unit_one, inv_one, gains[0])
    grad_input = (hidden_grad + norm_grad_one).reshape(images.shape)
    shared_count = owner_shared.shape[0]
    expert_count = owner_expert.shape[1]
    own_shared = shared_count // dp_size
    own_expert = expert_count // dp_size
    dp_index = lax.axis_index("dp")
    my_shared = lax.dynamic_slice_in_dim(owner_shared, dp_index * own_shared, own_shared)
    my_expert = lax.dynamic_slice_in_dim(owner_expert, dp_index * own_expert, own_expert, axis=1)
    shared_tiles = jnp.concatenate([to_tiles(qkv_weight_grad), to_tiles(out_grad)], axis=0)
    expert_tiles = jnp.concatenate([to_tiles(up_grad), to_tiles(down_grad)], axis=1)
    expert_perm = jnp.take_along_axis(expert_tiles, owner_expert[:, :, None, None], axis=1)
    gain_grads = jnp.stack([gain_grad_one, gain_grad_two], axis=0)
    shared_sum, router_total, gains_total = lax.psum(
        (shared_tiles, router_grad, gain_grads), ("dp", "expert")
    )
    shared_own = shared_sum[my_shared]
    expert_own = lax.psum_scatter(
        expert_perm.astype(jnp.bfloat16), "dp", scatter_dimension=1, tiled=True
    ).astype(jnp.float32)
    shared_old = jnp.concatenate([to_tiles(qkv_weight), to_tiles(out_weight)], axis=0)[
        my_shared
    ].astype(jnp.float32)
    expert_old = jnp.take_along_axis(
        jnp.concatenate([to_tiles(up_weight), to_tiles(down_weight)], axis=1),
        my_expert[:, :, None, None],
        axis=1,
    ).astype(jnp.float32)
    shared_m_new, shared_v_new, shared_w_new = rotated_adam(
        shared_own, shared_old, shared_m, shared_v, shared_left, shared_right
    )
    expert_m_new, expert_v_new, expert_w_new = rotated_adam(
        expert_own, expert_old, expert_m, expert_v, expert_left, expert_right
    )
    router_m_new, router_v_new, router_w_new = plain_adam(
        router_total, router_weight.astype(jnp.float32), router_m, router_v, (0, 1)
    )
    gains_m_new, gains_v_new, gains_w_new = plain_adam(gains_total, gains, gains_m, gains_v, (1,))
    shared_all, expert_all = (
        lax.all_gather(shared_w_new.astype(jnp.bfloat16), "dp", axis=0, tiled=True),
        lax.all_gather(expert_w_new.astype(jnp.bfloat16), "dp", axis=1, tiled=True),
    )
    qkv_count = model_width // TILE * (3 * model_width // TILE)
    up_count = model_width // TILE * (hidden_width // TILE)
    shared_inverse = (
        jnp.zeros((shared_count,), jnp.int32)
        .at[owner_shared]
        .set(jnp.arange(shared_count, dtype=jnp.int32))
    )
    shared_ordered = shared_all[shared_inverse]
    qkv_copy = from_tiles(shared_ordered[:qkv_count], model_width, 3 * model_width)
    out_copy = from_tiles(shared_ordered[qkv_count:], model_width, model_width)
    expert_rows = jnp.arange(local_experts, dtype=jnp.int32)[:, None]
    expert_inverse = (
        jnp.zeros((local_experts, expert_count), jnp.int32)
        .at[expert_rows, owner_expert]
        .set(jnp.arange(expert_count, dtype=jnp.int32)[None, :])
    )
    expert_ordered = jnp.take_along_axis(expert_all, expert_inverse[:, :, None, None], axis=1)
    up_copy = from_tiles(expert_ordered[:, :up_count], model_width, hidden_width)
    down_copy = from_tiles(expert_ordered[:, up_count:], hidden_width, model_width)
    return (
        out,
        grad_input,
        shared_m_new,
        shared_v_new,
        shared_w_new,
        expert_m_new,
        expert_v_new,
        expert_w_new,
        router_m_new,
        router_v_new,
        router_w_new,
        gains_m_new,
        gains_v_new,
        gains_w_new,
        qkv_copy,
        out_copy,
        up_copy,
        down_copy,
    )


def solution(mesh):
    return jax.shard_map(
        shards,
        mesh=mesh,
        in_specs=(
            P(("dp", "expert"), None, None),
            P(("dp", "expert"), None, None),
            P(),
            P(),
            P(),
            P(),
            P("expert", None, None),
            P("expert", None, None),
            P(("dp", "expert"), None, None),
            P(("dp", "expert"), None, None),
            P(),
            P("expert", None),
            P("dp", None, None),
            P("dp", None, None),
            P("dp", None, None),
            P("dp", None, None),
            P("expert", "dp", None, None),
            P("expert", "dp", None, None),
            P("expert", "dp", None, None),
            P("expert", "dp", None, None),
            P(),
            P(),
            P(),
            P(),
        ),
        out_specs=(
            P(("dp", "expert"), None, None),
            P(("dp", "expert"), None, None),
            P("dp", None, None),
            P("dp", None, None),
            P("dp", None, None),
            P("expert", "dp", None, None),
            P("expert", "dp", None, None),
            P("expert", "dp", None, None),
            P(),
            P(),
            P(),
            P(),
            P(),
            P(),
            P(),
            P(),
            P("expert", None, None),
            P("expert", None, None),
        ),
        check_vma=False,
    )
```

profile of v0, /device:TPU:0, one launch (start us, length us, event | category | flops | bytes accessed | tf_op | source)
XLA Modules:
  0.0 1101.2 jit_solution(5706929610592031100)
XLA Ops:
  37.0 11.8 %reshape.939 = bf16[4,196,3,12,64]{4,3,2,1,0:T(8,128)(2,1)} reshape(bf16[784,2304]{1,0:T(8,128)(2,1)} %convolution_convert_fusion) | data formatting | bytes 7225344 | tf_op jit(solution)/shard_map/reshape | solution.py:118
  48.9 12.5 %copy.344 = bf16[4,196,3,12,64]{1,4,3,0,2:T(8,128)(2,1)} copy(bf16[4,196,3,12,64]{4,3,2,1,0:T(8,128)(2,1)} %reshape.939) | data formatting | bytes 7225344 | tf_op jit(solution)/shard_map/reshape | solution.py:118
  86.8 9.0 gather_fusion
  108.6 13.7 %gather_fusion.10 = f32[1568]{0:T(1024)S(1)} fusion(f32[784,4]{0,1:T(4,128)S(1)} %fusion.107, s32[1568]{0:T(1024)S(1)} %reshape.877), kind=kCustom, calls=%fused_computation.10 | custom fusion | bytes 25088 | tf_op jit(solution)/shard_map/jit(take_along_axis)/gather | solution.py:155
  146.3 9.5 gather_fusion.2
  167.2 10.8 fusion.38
  184.8 54.4 %fusion.62 = bf16[4,412,768]{2,1,0:T(8,128)(2,1)} fusion(bf16[1,3072,768]{2,1,0:T(8,128)(2,1)} %param.31, f32[4,412,3072]{2,1,0:T(8,128)S(1)} %fusion.38), kind=kOutput, calls=%fused_computation.121 | convolution fusion | flops 8106577920 | bytes 27500544 | tf_op jit(solution)/shard_map/sjcf,jfd->sjcd/dot_general | solution.py:161
  243.8 55.7 %fusion.6 = bf16[4,1,412,3072]{3,2,0,1:T(8,128)(2,1)} fusion(f32[4,412,3072]{2,1,0:T(8,128)} %copy-done.8, bf16[4,412,768]{2,1,0:T(8,128)(2,1)} %all-to-all-done.2, bf16[1,3072,768]{2,1,0:T(8,128)(2,1)} %param.31), kind=kOutput, calls=%fused_computation.23 | convolution fusion | flops 8140750848 | bytes 37625856 | tf_op jit(solution)/shard_map/sjcd,jfd->sjcf/dot_general | solution.py:205
  299.5 46.1 %fusion.40 = bf16[3072,412,4]{0,1,2:T(8,128)(2,1)} fusion(f32[4,412,3072]{2,1,0:T(8,128)} %copy-done.8), kind=kLoop, calls=%fused_computation.83 | loop fusion | flops 329072640 | bytes 30375936 | tf_op jit(solution)/shard_map/sjcf,sjcd->jfd/dot_general | solution.py:209
  349.9 10.3 reshape.771
  360.3 13.4 %fusion.67 = bf16[4,412,768]{2,1,0:T(8,128)(2,1)} fusion(bf16[1,768,3072]{2,1,0:T(8,128)(2,1)} %param.30, bf16[4,1,412,3072]{3,2,0,1:T(8,128)(2,1)} %fusion.6), kind=kOutput, calls=%fused_computation.122 | convolution fusion | flops 7777505280 | bytes 17375232 | tf_op jit(solution)/shard_map/sjcf,jdf->sjcd/dot_general | solution.py:213
  378.3 13.7 %fusion.19 = bf16[8,384,2,384,1]{3,1,4,2,0:T(8,128)(2,1)} fusion(bf16[8,384,412,4,1]{1,0,2,3,4:T(8,128)(2,1)} %bitcast.400, bf16[2,384,412,4]{1,0,2,3:T(2,128)(2,1)} %dot_general.163), kind=kOutput, calls=%fused_computation.44 | convolution fusion | flops 7776239616 | bytes 17375232 | tf_op jit(solution)/shard_map/sjcf,sjcd->jfd/dot_general | solution.py:209
  396.3 10.3 dot_general.158
  413.0 9.5 gather_fusion.1
  429.0 13.7 %multiply_reduce_fusion.2 = (f32[784,2]{1,0:T(8,128)S(1)}, f32[784,768]{1,0:T(8,128)}) fusion(f32[784,2,768]{2,1,0:T(2,128)} %reshape.925, f32[784,768]{1,0:T(8,128)} %reshape.790, f32[784,2]{1,0:T(8,128)S(1)} %copy-done.22), kind=kLoop, calls=%fused_computation.70 | loop fusion | flops 4213216 | bytes 9646336 | tf_op jit(solution)/shard_map/reduce_sum | solution.py:179
  449.5 9.7 gather_fusion.3
  465.6 9.5 reduce_sum.208
  509.1 11.5 %multiply_convert_fusion = bf16[4,12,196,196]{2,3,1,0:T(8,128)(2,1)} fusion(f32[4,12,196,196]{2,3,1,0:T(8,128)} %get-tuple-element.184, f32[4,12,196,196]{2,3,1,0:T(8,128)} %copy-done.1, f32[4,12,196]{2,1,0:T(8,128)S(1)} %get-tuple-element.183, f32[4,12,196]{2,1,0:T(8,128)S(1)} %copy-done.31), kind=kLoop, calls=%fused_computation.53 | loop fusion | flops 9219840 | bytes 18514944 | tf_op jit(solution)/shard_map/convert_element_type | solution.py:250
  535.8 9.6 reshape.761
  575.7 12.2 %fusion.21 = bf16[2,384,8,384,1]{3,1,4,2,0:T(8,128)(2,1)S(1)} fusion(bf16[8,384,412,4]{1,0,2,3:T(8,128)(2,1)} %dot_general.158, bf16[2,384,412,4,1]{1,0,2,3,4:T(2,128)(2,1)} %bitcast.411), kind=kOutput, calls=%fused_computation.46 | convolution fusion | flops 7776239616 | bytes 17375232 | tf_op jit(solution)/shard_map/sjcd,sjcf->jdf/dot_general | solution.py:212
  592.2 10.0 gather_fusion.6
  602.2 10.7 fusion.18
  630.7 12.1 %copy.378 = bf16[2,6,384,384]{3,2,1,0:T(8,128)(2,1)} copy(bf16[2,6,384,384]{2,0,3,1:T(2,128)(2,1)} %bitcast.395) | data formatting | bytes 7077888 | tf_op jit(solution)/shard_map/transpose | solution.py:42
  651.4 181.8 %all-reduce.8.cloned.1.call-done = f32[16,384,384]{2,1,0:T(8,128)} async-done(((f32[16,384,384]{2,1,0:T(8,128)}), f32[16,384,384]{2,1,0:T(8,128)}) %all-reduce.8.cloned.1.call-update) | async-done | bytes 9437200 | tf_op jit(solution)/shard_map/psum | solution.py:282
  854.2 10.1 reshape.940
  886.9 9.7 maximum_bitcast_fusion.1
  947.9 45.8 %all-reduce.5 = (f32[768,4]{0,1:T(4,128)S(1)}, f32[2,768]{1,0:T(2,128)S(1)}) all-reduce(f32[768,4]{0,1:T(4,128)S(1)} %fusion.174, f32[2,768]{1,0:T(2,128)S(1)} %pad_maximum_fusion.2), channel_id=1, replica_groups=mesh['dp'=8,'expert'=4] {'dp','expert'}, use_global_device_ids=true, to_apply=%region_23.24 | all-reduce | flops 4608 | bytes 36864 | tf_op jit(solution)/shard_map/psum | solution.py:282
  1004.9 11.9 %copy.393 = bf16[2,6,384,384]{2,0,3,1:T(2,128)(2,1)} copy(bf16[2,6,384,384]{3,2,1,0:T(8,128)(2,1)} %bitcast.396) | data formatting | bytes 7077888 | tf_op jit(solution)/shard_map/reshape | solution.py:47
  1029.6 9.9 gather_fusion.9
  1047.9 9.0 fusion.167
  1056.9 9.3 copy.396
  1066.2 11.6 %reshape.788 = bf16[1,3072,768]{2,1,0:T(8,128)(2,1)} reshape(bf16[1,8,384,2,384]{4,3,2,1,0:T(2,128)(2,1)} %copy.396) | data formatting | bytes 9437184 | tf_op jit(solution)/shard_map/reshape | solution.py:48
  (369 shorter events, 404.3 us)
Async XLA Ops:
  8.0 899.3 %copy-start = (f32[1,4,384,384]{3,2,1,0:T(8,128)S(1)}, f32[1,4,384,384]{3,2,1,0:T(8,128)}, u32[]{:S(2)}) copy-start(f32[1,4,384,384]{3,2,1,0:T(8,128)} %param.43) | copy-start | bytes 7077892
  16.1 20.9 %copy-start.61 = (f32[768]{0:T(1024)}, f32[768]{0:T(1024)S(1)}, u32[]{:S(2)}) copy-start(f32[768]{0:T(1024)S(1)} %get-tuple-element.153) | copy-start | bytes 9220
  16.2 20.9 %copy-start.64 = (f32[784]{0:T(1024)}, f32[784]{0:T(1024)S(1)}, u32[]{:S(2)}) copy-start(f32[784]{0:T(1024)S(1)} %div.101) | copy-start | bytes 9412
  16.4 20.7 %copy-start.67 = (f32[784]{0:T(1024)}, f32[784]{0:T(1024)S(1)}, u32[]{:S(2)}) copy-start(f32[784]{0:T(1024)S(1)} %rsqrt.20) | copy-start | bytes 9412
  98.8 63.5 %all-to-all-start = ((bf16[4,412,768]{2,1,0:T(8,128)(2,1)}), bf16[4,412,768]{2,1,0:T(8,128)(2,1)}, u32[]{:S(2)}, u32[]{:S(2)}) async-start(bf16[4,412,768]{2,1,0:T(8,128)(2,1)} %reshape.749), calls=%async_computation | async-start | bytes 5111808 | tf_op jit(solution)/shard_map/all_to_all | solution.py:156
  123.2 38.2 %copy-start.32 = (pred[784,2]{1,0:T(8,128)(4,1)}, pred[784,2]{1,0:T(8,128)(4,1)S(1)}, u32[]{:S(2)}) copy-start(pred[784,2]{1,0:T(8,128)(4,1)S(1)} %copy.354) | copy-start | bytes 4708
  162.2 77.0 %all-to-all-start.2 = ((bf16[4,412,768]{2,1,0:T(8,128)(2,1)}), bf16[4,412,768]{2,1,0:T(8,128)(2,1)}, u32[]{:S(2)}, u32[]{:S(2)}) async-start(bf16[4,412,768]{2,1,0:T(8,128)(2,1)} %reshape.757), calls=%async_computation.2 | async-start | bytes 5111808 | tf_op jit(solution)/shard_map/all_to_all | solution.py:197
  239.2 134.4 %all-to-all-start.1 = ((bf16[4,412,768]{2,1,0:T(8,128)(2,1)}), bf16[4,412,768]{2,1,0:T(8,128)(2,1)}, u32[]{:S(2)}, u32[]{:S(2)}) async-start(bf16[4,412,768]{2,1,0:T(8,128)(2,1)} %fusion.62), calls=%async_computation.1 | async-start | bytes 5111808 | tf_op jit(solution)/shard_map/all_to_all | solution.py:164
  373.7 69.4 %all-to-all-start.3 = ((bf16[4,412,768]{2,1,0:T(8,128)(2,1)}), bf16[4,412,768]{2,1,0:T(8,128)(2,1)}, u32[]{:S(2)}, u32[]{:S(2)}) async-start(bf16[4,412,768]{2,1,0:T(8,128)(2,1)} %fusion.67), calls=%async_computation.3 | async-start | bytes 5111808 | tf_op jit(solution)/shard_map/all_to_all | solution.py:216
  378.2 455.0 %all-reduce.8.cloned.1.call-start = ((), (), s32[]{:S(2)}) async-start(), calls=%async_computation.5 | async-start | bytes 18874368 | tf_op jit(solution)/shard_map/psum | solution.py:282
  429.0 13.8 %copy-start.33 = (pred[784,2]{1,0:T(8,128)(4,1)S(1)}, pred[784,2]{1,0:T(8,128)(4,1)}, u32[]{:S(2)}) copy-start(pred[784,2]{1,0:T(8,128)(4,1)} %copy-done.32) | copy-start | bytes 4708
  429.0 14.0 %copy-start.56 = (s32[784,2]{0,1:T(2,128)S(1)}, s32[784,2]{0,1:T(2,128)}, u32[]{:S(2)}) copy-start(s32[784,2]{0,1:T(2,128)} %copy-done.55) | copy-start | bytes 18820
  429.0 14.0 %copy-start.37 = (f32[784,4]{0,1:T(4,128)S(1)}, f32[784,4]{0,1:T(4,128)}, u32[]{:S(2)}) copy-start(f32[784,4]{0,1:T(4,128)} %copy-done.36) | copy-start | bytes 37636
  429.0 14.0 %copy-start.43 = (f32[784]{0:T(1024)S(1)}, f32[784]{0:T(1024)}, u32[]{:S(2)}) copy-start(f32[784]{0:T(1024)} %copy-done.42) | copy-start | bytes 9412
  429.0 14.0 %copy-start.54 = (f32[784]{0:T(1024)S(1)}, f32[784]{0:T(1024)}, u32[]{:S(2)}) copy-start(f32[784]{0:T(1024)} %copy-done.53) | copy-start | bytes 9412
  443.1 32.0 %copy-start.57 = (bf16[784,4]{0,1:T(4,128)(2,1)}, bf16[784,4]{0,1:T(4,128)(2,1)S(1)}, u32[]{:S(2)}) copy-start(bf16[784,4]{0,1:T(4,128)(2,1)S(1)} %multiply_convert_fusion.6) | copy-start | bytes 18820
  575.6 12.3 %slice-start.1 = ((s8[4718592]{0:T(1024)(128)(4,1)}), s8[524288]{0:T(1024)(128)(4,1)S(1)}, s32[]{:S(2)}) async-start(s8[4718592]{0:T(1024)(128)(4,1)} %bitcast.406), calls=%async_computation.10 | async-start | bytes 1048576
  575.6 327.1 %reduce-scatter.2.cloned.1.call-start = ((), (), s32[]{:S(2)}) async-start(), calls=%async_computation.6 | async-start | bytes 10616832 | tf_op jit(solution)/shard_map/reduce_scatter | solution.py:286
  575.7 12.3 %slice-start.2 = ((s8[4718592]{0:T(1024)(128)(4,1)}), s8[4194304]{0:T(1024)(128)(4,1)S(1)}, s32[]{:S(2)}) async-start(s8[4718592]{0:T(1024)(128)(4,1)} %bitcast.406), calls=%async_computation.11 | async-start | bytes 8388608
  612.9 382.1 %all-gather.4.cloned.1.call-start = ((), (), s32[]{:S(2)}) async-start(), calls=%async_computation.7 | async-start | bytes 5308416 | tf_op jit(solution)/shard_map/all_gather | solution.py:308
  630.7 12.1 %copy-start.86 = (s32[16]{0:T(128)S(1)}, s32[16]{0:T(128)}, u32[]{:S(2)}) copy-start(s32[16]{0:T(128)} %param.34) | copy-start | bytes 196
  854.2 175.4 %all-gather.6.cloned.1.call-start = ((), (), s32[]{:S(2)}) async-start(), calls=%async_computation.8 | async-start | bytes 10616832 | tf_op jit(solution)/shard_map/all_gather | solution.py:309
  918.1 11.3 %copy-start.60 = (f32[2,768]{1,0:T(2,128)S(1)}, f32[2,768]{1,0:T(2,128)}, u32[]{:S(2)}) copy-start(f32[2,768]{1,0:T(2,128)} %param.26) | copy-start | bytes 18436
  924.7 11.3 %copy-start.74 = (f32[784]{0:T(1024)S(1)}, f32[784]{0:T(1024)}, u32[]{:S(2)}) copy-start(f32[784]{0:T(1024)} %get-tuple-element.145) | copy-start | bytes 9412
  924.7 11.3 %copy-start.73 = (f32[784]{0:T(1024)S(1)}, f32[784]{0:T(1024)}, u32[]{:S(2)}) copy-start(f32[784]{0:T(1024)} %get-tuple-element.151) | copy-start | bytes 9412
  924.7 11.3 %copy-start.63 = (f32[768]{0:T(1024)S(1)}, f32[768]{0:T(1024)}, u32[]{:S(2)}) copy-start(f32[768]{0:T(1024)} %copy-done.61) | copy-start | bytes 9220
  924.7 11.3 %copy-start.66 = (f32[784]{0:T(1024)S(1)}, f32[784]{0:T(1024)}, u32[]{:S(2)}) copy-start(f32[784]{0:T(1024)} %copy-done.64) | copy-start | bytes 9412
  924.8 11.3 %copy-start.69 = (f32[784]{0:T(1024)S(1)}, f32[784]{0:T(1024)}, u32[]{:S(2)}) copy-start(f32[784]{0:T(1024)} %copy-done.67) | copy-start | bytes 9412
  940.6 53.1 %copy-start.77 = (f32[2,768]{1,0:T(2,128)S(1)}, f32[2,768]{1,0:T(2,128)}, u32[]{:S(2)}) copy-start(f32[2,768]{1,0:T(2,128)} %param.47) | copy-start | bytes 18436
  940.6 53.1 %copy-start.78 = (f32[2,768]{1,0:T(2,128)S(1)}, f32[2,768]{1,0:T(2,128)}, u32[]{:S(2)}) copy-start(f32[2,768]{1,0:T(2,128)} %param.46) | copy-start | bytes 18436
  940.6 53.8 %copy-start.75 = (f32[768,4]{0,1:T(4,128)S(1)}, f32[768,4]{0,1:T(4,128)}, u32[]{:S(2)}) copy-start(f32[768,4]{0,1:T(4,128)} %param.45) | copy-start | bytes 36868
  940.6 53.7 %copy-start.76 = (f32[768,4]{0,1:T(4,128)S(1)}, f32[768,4]{0,1:T(4,128)}, u32[]{:S(2)}) copy-start(f32[768,4]{0,1:T(4,128)} %param.44) | copy-start | bytes 36868
  (66 other events, 359.4 us)
Sparse Core Ops, SparseCore 0:
  575.8 257.3 all-reduce.7
Sparse Core Ops, SparseCore 1:
  613.0 121.0 reduce-scatter.1
  854.3 51.1 all-gather.3
  924.9 91.7 all-gather.5
where the time goes:
time: 1110 us; the launch traced here: 1100 us
  local copies, waits for them, and re-layouts  415 us (37%)
  matrix products  264 us (24%)
  waiting for transfers between devices  182 us (16%)
  other arithmetic  157 us (14%)
  blocking collectives  45.8 us (4%)
  starting transfers between devices  19.6 us (2%)
  between operations  18 us (2%)
    psum x1, waiting for transfers between devices, shards(): lax.psum((shared_tiles, router_grad, gain_grads), ('dp', 'expert'))  182 us
    dot_general x1, matrix products, shards(): jnp.einsum('sjcd,jfd->sjcf', grouped_grad, down_weight, preferred_element...  55.7 us
    dot_general x1, matrix products, shards(): jnp.einsum('sjcf,jfd->sjcd', activated, down_weight, preferred_element_ty...  54.4 us
    dot_general x1, other arithmetic, shards(): jnp.einsum('sjcf,sjcd->jfd', act_low, grouped_grad, preferred_element_typ...  46.1 us
    psum x1, blocking collectives, shards(): lax.psum((shared_tiles, router_grad, gain_grads), ('dp', 'expert'))  45.8 us
    unnamed x190, local copies, waits for them, and re-layouts  43 us
    reshape x4, local copies, waits for them, and re-layouts, to_tiles(): matrix.reshape(leading + (row_count // TILE, TILE, col_count // TILE, TILE))  28.2 us
    reshape x2, local copies, waits for them, and re-layouts, shards(): qkv_rows.reshape(image_count, patch_count, 3, HEADS, HEAD_DIM)  24.3 us
  transfers between devices with their start and end apart: 8, of which 1 were waited for; matrix products, arithmetic and copies ran while one was open for 49% of the time, Pallas kernels for 0%

commit v1 on v0

v1 whole, which is shorter than its diff:
```python
import functools

import jax
import jax.numpy as jnp
from jax import lax
from jax.experimental import pallas as pl
from jax.experimental.pallas import tpu as pltpu
from jax.sharding import PartitionSpec as P

HEADS = 12
HEAD_DIM = 64
TILE = 384
LANES = 128
PAIRS = HEADS * HEAD_DIM // LANES

norm_eps = 1e-06
adam_beta = 0.5
adam_eps = 1e-08
adam_step = 5
rate_scale = 0.3
correction = 1.0 - adam_beta**adam_step
score_scale = HEAD_DIM ** (-0.5)

f32 = jnp.float32
bf16 = jnp.bfloat16
VMEM_LIMIT = 60 * 1024 * 1024


def round_up(value, step):
    return (value + step - 1) // step * step


def dot_nn(left, right):
    return lax.dot_general(left, right, (((1,), (0,)), ((), ())), preferred_element_type=f32)


def dot_nt(left, right):
    return lax.dot_general(left, right, (((1,), (1,)), ((), ())), preferred_element_type=f32)


def dot_tn(left, right):
    return lax.dot_general(left, right, (((0,), (0,)), ((), ())), preferred_element_type=f32)


def params(limit=VMEM_LIMIT):
    return pltpu.CompilerParams(vmem_limit_bytes=limit, dimension_semantics=("arbitrary",))


def norm_stats(values):
    center = values - jnp.mean(values, axis=-1, keepdims=True)
    inv_std = lax.rsqrt(jnp.mean(center * center, axis=-1, keepdims=True) + norm_eps)
    return center * inv_std, inv_std


def norm_back(grad_normed, unit_rows, inv_std, gain_row):
    grad_hat = grad_normed * gain_row
    gain_grad = jnp.sum(grad_normed * unit_rows, axis=0, keepdims=True)
    mean_one = jnp.mean(grad_hat, axis=-1, keepdims=True)
    mean_two = jnp.mean(grad_hat * unit_rows, axis=-1, keepdims=True)
    return inv_std * (grad_hat - mean_one - unit_rows * mean_two), gain_grad


def gelu_pair(x):
    t = 1.0 / (1.0 + 0.23164188 * jnp.abs(x))
    bell = jnp.exp(-0.5 * (x * x))
    poly = t * (
        0.127414796 + t * (-0.142248368 + t * (0.7107068705 + t * (-0.7265760135 + t * 0.5307027145)))
    )
    tail = poly * bell
    phi = jnp.where(x >= 0.0, 1.0 - tail, tail)
    return x * phi, phi + x * (bell * 0.3989422804014327)


def one_hot(columns, width):
    return jnp.where(
        columns == lax.broadcasted_iota(jnp.int32, (columns.shape[0], width), 1), 1.0, 0.0
    ).astype(bf16)


def full(shape):
    return pl.BlockSpec(shape, lambda i, *_: (0,) * len(shape))


def per(shape):
    return pl.BlockSpec((1,) + shape, lambda i, *_: (i,) + (0,) * len(shape))


def front_body(
    img, cot, gains, qkv_w, out_w, router_w, qkv_o, attn_o, mixed_o, hid_o, routed_o, probs_o, up_o, rows,
    *, patches, experts
):
    padded = rows.shape[0]
    rows[...] = jnp.zeros(rows.shape, f32)
    rows[0:patches, :] = cot[0].astype(f32)
    up_o[0] = rows[...].astype(bf16)
    rows[0:patches, :] = img[0].astype(f32)
    tokens = rows[...]
    unit, _ = norm_stats(tokens)
    normed = (unit * gains[0:1, :]).astype(bf16)
    qkv_o[0] = dot_nn(normed, qkv_w[...]).astype(bf16)
    width = PAIRS * LANES
    low_half = lax.broadcasted_iota(jnp.int32, (1, LANES), 1) < HEAD_DIM
    halves = (low_half.astype(f32).astype(bf16), (1.0 - low_half.astype(f32)).astype(bf16))
    key_bias = jnp.where(lax.broadcasted_iota(jnp.int32, (1, padded), 1) < patches, 0.0, -1e30)
    for pair in range(PAIRS):
        q = qkv_o[0, :, pair * LANES : (pair + 1) * LANES]
        k = qkv_o[0, :, width + pair * LANES : width + (pair + 1) * LANES]
        v = qkv_o[0, :, 2 * width + pair * LANES : 2 * width + (pair + 1) * LANES]
        outs = []
        for half in range(2):
            scores = dot_nt(q * halves[half], k) * score_scale + key_bias
            expo = jnp.exp(scores - jnp.max(scores, axis=-1, keepdims=True))
            low = (expo * (1.0 / jnp.sum(expo, axis=-1, keepdims=True))).astype(bf16)
            attn_o[0, 2 * pair + half] = low
            outs.append(dot_nn(low, v))
        mixed_o[0, :, pair * LANES : (pair + 1) * LANES] = jnp.where(low_half, outs[0], outs[1]).astype(bf16)
    hidden = rows[...] + dot_nn(mixed_o[0], out_w[...])
    hid_o[0] = hidden
    unit_two, _ = norm_stats(hidden)
    routed = (unit_two * gains[1:2, :]).astype(bf16)
    routed_o[0] = routed
    logits = dot_nn(routed, router_w[...])
    logits = jnp.where(lax.broadcasted_iota(jnp.int32, logits.shape, 1) < experts, logits, -1e30)
    expo = jnp.exp(logits - jnp.max(logits, axis=-1, keepdims=True))
    probs_o[0] = expo / jnp.sum(expo, axis=-1, keepdims=True)


def front(images, cotangent, gains, qkv_w, out_w, router_pad, experts, padded):
    count, patches, width = images.shape
    return pl.pallas_call(
        functools.partial(front_body, patches=patches, experts=experts),
        grid=(count,),
        in_specs=[
            per((patches, width)),
            per((patches, width)),
            full(gains.shape),
            full(qkv_w.shape),
            full(out_w.shape),
            full(router_pad.shape),
        ],
        out_specs=[
            per((padded, 3 * width)),
            per((HEADS, padded, padded)),
            per((padded, width)),
            per((padded, width)),
            per((padded, width)),
            per((padded, LANES)),
            per((padded, width)),
        ],
        out_shape=[
            jax.ShapeDtypeStruct((count, padded, 3 * width), bf16),
            jax.ShapeDtypeStruct((count, HEADS, padded, padded), bf16),
            jax.ShapeDtypeStruct((count, padded, width), bf16),
            jax.ShapeDtypeStruct((count, padded, width), f32),
            jax.ShapeDtypeStruct((count, padded, width), bf16),
            jax.ShapeDtypeStruct((count, padded, LANES), f32),
            jax.ShapeDtypeStruct((count, padded, width), bf16),
        ],
        scratch_shapes=[pltpu.VMEM((padded, width), f32)],
        compiler_params=params(),
        name="front",
    )(images, cotangent, gains, qkv_w, out_w, router_pad)


def dispatch_body(choice_rows, slot_rows, routed, probs, upstream, x_o, g_o):
    expert = pl.program_id(0)
    places = x_o.shape[1]
    tokens = routed.shape[0]
    slot = jnp.where(
        choice_rows[0:1, :] == expert,
        slot_rows[0:1, :],
        jnp.where(choice_rows[1:2, :] == expert, slot_rows[1:2, :], -1),
    )
    table = jnp.where(
        slot == lax.broadcasted_iota(jnp.int32, (places, tokens), 0), 1.0, 0.0
    ).astype(bf16)
    x_o[0] = dot_nn(table, routed[...]).astype(bf16)
    lane = lax.broadcasted_iota(jnp.int32, (1, LANES), 1)
    gate = jnp.sum(jnp.where(lane == expert, probs[...], 0.0), axis=-1, keepdims=True)
    gated = (gate * upstream[...].astype(f32)).astype(bf16)
    g_o[0] = dot_nn(table, gated).astype(bf16)


def dispatch(choice_rows, slot_rows, routed, probs, upstream, experts, places):
    width = routed.shape[1]
    shape = jax.ShapeDtypeStruct((experts, places, width), bf16)
    return pl.pallas_call(
        dispatch_body,
        grid=(experts,),
        in_specs=[full(a.shape) for a in (choice_rows, slot_rows, routed, probs, upstream)],
        out_specs=[per((places, width)), per((places, width))],
        out_shape=[shape, shape],
        compiler_params=params(),
        name="dispatch",
    )(choice_rows, slot_rows, routed, probs, upstream)


FF_CHUNK = 512


def ffn_fwd_body(x, up_w, down_w, act_o, slope_o, y_o):
    hidden = up_w.shape[2]
    total = None
    for start in range(0, hidden, FF_CHUNK):
        part = slice(start, start + FF_CHUNK)
        act, slope = gelu_pair(dot_nn(x[...], up_w[0, :, part]))
        act = act.astype(bf16)
        act_o[:, part] = act
        slope_o[:, part] = slope.astype(bf16)
        piece = dot_nn(act, down_w[0, part, :])
        total = piece if total is None else total + piece
    y_o[...] = total.astype(bf16)


def ffn_bwd_body(g, slope, up_w, down_w, pre_o, in_o):
    hidden = up_w.shape[2]
    total = None
    for start in range(0, hidden, FF_CHUNK):
        part = slice(start, start + FF_CHUNK)
        pre = (dot_nt(g[...], down_w[0, part, :]) * slope[:, part].astype(f32)).astype(bf16)
        pre_o[:, part] = pre
        piece = dot_nt(pre, up_w[0, :, part])
        total = piece if total is None else total + piece
    in_o[...] = total.astype(bf16)


def row_blocks(rows, width):
    return pl.BlockSpec((rows, width), lambda i: (i, 0))


def ffn_fwd(x, up_w, down_w):
    rows, width = x.shape
    hidden = up_w.shape[2]
    block = rows // 4
    return pl.pallas_call(
        ffn_fwd_body,
        grid=(4,),
        in_specs=[row_blocks(block, width), full(up_w.shape), full(down_w.shape)],
        out_specs=[row_blocks(block, hidden), row_blocks(block, hidden), row_blocks(block, width)],
        out_shape=[
            jax.ShapeDtypeStruct((rows, hidden), bf16),
            jax.ShapeDtypeStruct((rows, hidden), bf16),
            jax.ShapeDtypeStruct((rows, width), bf16),
        ],
        compiler_params=params(),
        name="ffn_fwd",
    )(x, up_w, down_w)


def ffn_bwd(g, slope, up_w, down_w):
    rows, width = g.shape
    hidden = up_w.shape[2]
    block = rows // 4
    return pl.pallas_call(
        ffn_bwd_body,
        grid=(4,),
        in_specs=[
            row_blocks(block, width),
            row_blocks(block, hidden),
            full(up_w.shape),
            full(down_w.shape),
        ],
        out_specs=[row_blocks(block, hidden), row_blocks(block, width)],
        out_shape=[
            jax.ShapeDtypeStruct((rows, hidden), bf16),
            jax.ShapeDtypeStruct((rows, width), bf16),
        ],
        compiler_params=params(),
        name="ffn_bwd",
    )(g, slope, up_w, down_w)


def expert_dw_body(owner, x, g, act, pre, tile_o, *, up_cols, down_cols, up_count):
    tile = owner[pl.program_id(0)]

    @pl.when(tile < up_count)
    def _():
        row = pl.multiple_of(tile // up_cols * TILE, TILE)
        tile_o[0] = dot_tn(x[:, pl.ds(row, TILE)], pre[...]).astype(bf16)

    @pl.when(tile >= up_count)
    def _():
        col = pl.multiple_of((tile - up_count) % down_cols * TILE, TILE)
        tile_o[0] = dot_tn(act[...], g[:, pl.ds(col, TILE)]).astype(bf16)


def expert_dw(owner, x, g, act, pre):
    rows, width = x.shape
    hidden = act.shape[1]
    up_cols = hidden // TILE
    down_cols = width // TILE
    up_count = up_cols * down_cols
    count = owner.shape[0]

    def pre_at(i, owner):
        tile = owner[i]
        return (0, jnp.where(tile < up_count, tile % up_cols, 0))

    def act_at(i, owner):
        tile = owner[i]
        return (0, jnp.where(tile >= up_count, (tile - up_count) // down_cols, 0))

    return pl.pallas_call(
        functools.partial(expert_dw_body, up_cols=up_cols, down_cols=down_cols, up_count=up_count),
        grid_spec=pltpu.PrefetchScalarGridSpec(
            num_scalar_prefetch=1,
            grid=(count,),
            in_specs=[
                full((rows, width)),
                full((rows, width)),
                pl.BlockSpec((rows, TILE), act_at),
                pl.BlockSpec((rows, TILE), pre_at),
            ],
            out_specs=per((TILE, TILE)),
        ),
        out_shape=jax.ShapeDtypeStruct((count, TILE, TILE), bf16),
        compiler_params=params(),
        name="expert_dw",
    )(owner, x, g, act, pre)


def combine_body(choice, slot, returned, hidden, upstream, probs, routed, out_o, logit_o, router_o, *, patches):
    experts, places = returned.shape[0], returned.shape[1]
    up = upstream[0].astype(f32)
    prob = probs[0]
    lane = lax.broadcasted_iota(jnp.int32, (1, LANES), 1)
    total = hidden[0]
    prob_grad = jnp.zeros(prob.shape, f32)
    for expert in range(experts):
        column = jnp.where(
            choice[0, :, 0:1] == expert,
            slot[0, :, 0:1],
            jnp.where(choice[0, :, 1:2] == expert, slot[0, :, 1:2], -1),
        )
        rows = dot_nn(one_hot(column, places), returned[expert])
        total = total + prob[:, expert : expert + 1] * rows
        prob_grad = prob_grad + jnp.where(
            lane == expert, jnp.sum(up * rows, axis=-1, keepdims=True), 0.0
        )
    out_o[0] = total[0:patches, :].astype(bf16)
    inner = jnp.sum(prob * prob_grad, axis=-1, keepdims=True)
    logit = (prob * (prob_grad - inner)).astype(bf16)
    logit_o[0] = logit

    @pl.when(pl.program_id(0) == 0)
    def _():
        router_o[...] = jnp.zeros(router_o.shape, f32)

    router_o[...] += dot_tn(logit, routed[0])


def combine(choice, slot, returned, hidden, upstream, probs, routed, patches):
    count, padded, width = hidden.shape
    return pl.pallas_call(
        functools.partial(combine_body, patches=patches),
        grid=(count,),
        in_specs=[
            per((padded, 2)),
            per((padded, 2)),
            full(returned.shape),
            per((padded, width)),
            per((padded, width)),
            per((padded, LANES)),
            per((padded, width)),
        ],
        out_specs=[per((patches, width)), per((padded, LANES)), full((LANES, width))],
        out_shape=[
            jax.ShapeDtypeStruct((count, patches, width), bf16),
            jax.ShapeDtypeStruct((count, padded, LANES), bf16),
            jax.ShapeDtypeStruct((LANES, width), f32),
        ],
        compiler_params=params(),
        name="combine",
    )(choice, slot, returned, hidden, upstream, probs, routed)


def back_body(
    owner, choice, slot, returned, logit, router_w, hidden, upstream, gains, out_w, mixed, qkv, attn, qkv_w, img,
    grad_o, tile_o, gain_o,
    rows, normed_all, qkv_grad_all, mixed_all, branch_all, mixed_grad_s, hidden_grad_s,
    *, patches, places
):
    image = pl.program_id(0)
    padded, width = rows.shape
    base = pl.multiple_of(image * padded, 16)
    here = pl.ds(base, padded)
    place = jnp.where(slot[0] >= 0, choice[0] * places + slot[0], -1)
    grid_places = lax.broadcasted_iota(jnp.int32, (padded, returned.shape[0]), 1)
    hits = (place[:, 0:1] == grid_places) | (place[:, 1:2] == grid_places)
    table = jnp.where(hits, 1.0, 0.0).astype(bf16)
    routed_grad = dot_nt(logit[0], router_w[...]) + dot_nn(table, returned[...])
    unit_two, inv_two = norm_stats(hidden[0])
    norm_grad, gain_two = norm_back(routed_grad, unit_two, inv_two, gains[1:2, :])
    hidden_grad = upstream[0].astype(f32) + norm_grad
    hidden_grad_s[...] = hidden_grad
    branch = hidden_grad.astype(bf16)
    branch_all[here, :] = branch
    mixed_all[here, :] = mixed[0]
    mixed_grad_s[...] = dot_nt(branch, out_w[...]).astype(bf16)
    low_half = lax.broadcasted_iota(jnp.int32, (1, LANES), 1) < HEAD_DIM
    halves = (low_half.astype(f32).astype(bf16), (1.0 - low_half.astype(f32)).astype(bf16))
    for pair in range(PAIRS):
        cols = slice(pair * LANES, (pair + 1) * LANES)
        q = qkv[0, :, pair * LANES : (pair + 1) * LANES]
        k = qkv[0, :, width + pair * LANES : width + (pair + 1) * LANES]
        v = qkv[0, :, 2 * width + pair * LANES : 2 * width + (pair + 1) * LANES]
        mg = mixed_grad_s[:, cols]
        q_grads, k_grads, v_grads = [], [], []
        for half in range(2):
            low = attn[0, 2 * pair + half]
            weights = low.astype(f32)
            weight_grad = dot_nt(mg * halves[half], v)
            product = weights * weight_grad
            inner = jnp.sum(product, axis=-1, keepdims=True)
            score = (product - weights * inner).astype(bf16)
            q_grads.append(dot_nn(score, k))
            k_grads.append(dot_tn(score, q))
            v_grads.append(dot_tn(low, mg))
        qkv_grad_all[here, pair * LANES : (pair + 1) * LANES] = (
            jnp.where(low_half, q_grads[0], q_grads[1]) * score_scale
        ).astype(bf16)
        qkv_grad_all[here, width + pair * LANES : width + (pair + 1) * LANES] = (
            jnp.where(low_half, k_grads[0], k_grads[1]) * score_scale
        ).astype(bf16)
        qkv_grad_all[here, 2 * width + pair * LANES : 2 * width + (pair + 1) * LANES] = jnp.where(
            low_half, v_grads[0], v_grads[1]
        ).astype(bf16)
    rows[...] = jnp.zeros(rows.shape, f32)
    rows[0:patches, :] = img[0].astype(f32)
    unit_one, inv_one = norm_stats(rows[...])
    normed_all[here, :] = (unit_one * gains[0:1, :]).astype(bf16)
    normed_grad = dot_nt(qkv_grad_all[here, :], qkv_w[...])
    norm_grad_one, gain_one = norm_back(normed_grad, unit_one, inv_one, gains[0:1, :])
    grad_o[0] = (hidden_grad_s[...] + norm_grad_one)[0:patches, :]

    @pl.when(image == 0)
    def _():
        gain_o[...] = jnp.zeros(gain_o.shape, f32)

    gain_o[0:1, :] += gain_one
    gain_o[1:2, :] += gain_two

    @pl.when(image == pl.num_programs(0) - 1)
    def _():
        row_tiles = width // TILE
        qkv_cols = 3 * row_tiles
        qkv_count = row_tiles * qkv_cols

        def one(s, carry):
            tile = owner[s]

            @pl.when(tile < qkv_count)
            def _():
                row = pl.multiple_of(tile // qkv_cols * TILE, TILE)
                col = pl.multiple_of(tile % qkv_cols * TILE, TILE)
                tile_o[s] = dot_tn(
                    normed_all[:, pl.ds(row, TILE)], qkv_grad_all[:, pl.ds(col, TILE)]
                ).astype(bf16)

            @pl.when(tile >= qkv_count)
            def _():
                rest = tile - qkv_count
                row = pl.multiple_of(rest // row_tiles * TILE, TILE)
                col = pl.multiple_of(rest % row_tiles * TILE, TILE)
                tile_o[s] = dot_tn(
                    mixed_all[:, pl.ds(row, TILE)], branch_all[:, pl.ds(col, TILE)]
                ).astype(bf16)

            return carry

        lax.fori_loop(0, tile_o.shape[0], one, 0)


def back(owner, choice, slot, returned, logit, router_pad, hidden, upstream, gains, out_w, mixed, qkv, attn, qkv_w,
         images, places):
    count, patches, width = images.shape
    padded = hidden.shape[1]
    tiles = owner.shape[0]
    return pl.pallas_call(
        functools.partial(back_body, patches=patches, places=places),
        grid_spec=pltpu.PrefetchScalarGridSpec(
            num_scalar_prefetch=1,
            grid=(count,),
            in_specs=[
                per((padded, 2)),
                per((padded, 2)),
                full(returned.shape),
                per((padded, LANES)),
                full(router_pad.shape),
                per((padded, width)),
                per((padded, width)),
                full(gains.shape),
                full(out_w.shape),
                per((padded, width)),
                per((padded, 3 * width)),
                per((HEADS, padded, padded)),
                full(qkv_w.shape),
                per((patches, width)),
            ],
            out_specs=[per((patches, width)), full((tiles, TILE, TILE)), full((8, width))],
            scratch_shapes=[
                pltpu.VMEM((padded, width), f32),
                pltpu.VMEM((count * padded, width), bf16),
                pltpu.VMEM((count * padded, 3 * width), bf16),
                pltpu.VMEM((count * padded, width), bf16),
                pltpu.VMEM((count * padded, width), bf16),
                pltpu.VMEM((padded, width), bf16),
                pltpu.VMEM((padded, width), f32),
            ],
        ),
        out_shape=[
            jax.ShapeDtypeStruct((count, patches, width), f32),
            jax.ShapeDtypeStruct((tiles, TILE, TILE), bf16),
            jax.ShapeDtypeStruct((8, width), f32),
        ],
        compiler_params=params(),
        name="back",
    )(owner, choice, slot, returned, logit, router_pad, hidden, upstream, gains, out_w, mixed, qkv, attn, qkv_w, images)


def adam_body(owner, grad, w_one, w_two, m, v, left, right, m_o, v_o, w_o, low_o, *, first_count):
    tile = owner[pl.program_id(0)]
    first = (tile < first_count).astype(f32)
    old = w_one[...].astype(f32) * first + w_two[...].astype(f32) * (1.0 - first)
    left_low = left[0].astype(bf16)
    right_low = right[0].astype(bf16)
    turned = dot_nn(dot_tn(left_low, grad[0].astype(bf16)).astype(bf16), right_low)
    m_new = adam_beta * m[0] + (1.0 - adam_beta) * turned
    v_new = adam_beta * v[0] + (1.0 - adam_beta) * turned * turned
    m_o[0] = m_new
    v_o[0] = v_new
    direction = m_new / correction / (jnp.sqrt(v_new / correction) + adam_eps)
    back_turn = dot_nt(dot_nn(left_low, direction.astype(bf16)).astype(bf16), right_low)
    rate = rate_scale * jnp.sqrt(jnp.mean(old * old))
    new = old - rate * back_turn
    w_o[0] = new
    low_o[0] = new.astype(bf16)


def rotated_adam(owner, grad, w_one, w_two, m, v, left, right):
    count = m.shape[0]
    one_cols = w_one.shape[1] // TILE
    two_cols = w_two.shape[1] // TILE
    first_count = w_one.shape[0] // TILE * one_cols

    def one_at(i, owner):
        tile = jnp.minimum(owner[i], first_count - 1)
        return (tile // one_cols, tile % one_cols)

    def two_at(i, owner):
        tile = jnp.maximum(owner[i] - first_count, 0)
        return (tile // two_cols, tile % two_cols)

    spec = per((TILE, TILE))
    shape = jax.ShapeDtypeStruct((count, TILE, TILE), f32)
    return pl.pallas_call(
        functools.partial(adam_body, first_count=first_count),
        grid_spec=pltpu.PrefetchScalarGridSpec(
            num_scalar_prefetch=1,
            grid=(count,),
            in_specs=[
                spec,
                pl.BlockSpec((TILE, TILE), one_at),
                pl.BlockSpec((TILE, TILE), two_at),
                spec,
                spec,
                spec,
                spec,
            ],
            out_specs=[spec, spec, spec, spec],
        ),
        out_shape=[shape, shape, shape, jax.ShapeDtypeStruct((count, TILE, TILE), bf16)],
        compiler_params=params(),
        name="adam",
    )(owner, grad, w_one, w_two, m, v, left, right)


def untile_body(slot_of, tile, out):
    out[...] = tile[0]


def untile(slot_of, tiles, row_count, col_count):
    cols = col_count // TILE
    count = slot_of.shape[0]
    return pl.pallas_call(
        untile_body,
        grid_spec=pltpu.PrefetchScalarGridSpec(
            num_scalar_prefetch=1,
            grid=(count,),
            in_specs=[pl.BlockSpec((1, TILE, TILE), lambda i, slot_of: (slot_of[i], 0, 0))],
            out_specs=pl.BlockSpec((TILE, TILE), lambda i, slot_of: (i // cols, i % cols)),
        ),
        out_shape=jax.ShapeDtypeStruct((row_count, col_count), bf16),
        compiler_params=params(),
        name="untile",
    )(slot_of, tiles)


def inverse(owner):
    ids = jnp.arange(owner.shape[0], dtype=jnp.int32)
    return jnp.sum(jnp.where(owner[None, :] == ids[:, None], ids[None, :], 0), axis=1)


def plain_adam(grad_values, weight_values, first_moment, second_moment, axes):
    first_new = adam_beta * first_moment + (1.0 - adam_beta) * grad_values
    second_new = adam_beta * second_moment + (1.0 - adam_beta) * grad_values * grad_values
    direction = first_new / correction / (jnp.sqrt(second_new / correction) + adam_eps)
    step_rate = rate_scale * jnp.sqrt(
        jnp.mean(weight_values * weight_values, axis=axes, keepdims=True)
    )
    return (first_new, second_new, weight_values - step_rate * direction)


def shards(
    images,
    cotangent,
    gains,
    qkv_weight,
    out_weight,
    router_weight,
    up_weight,
    down_weight,
    choices,
    slots,
    owner_shared,
    owner_expert,
    shared_m,
    shared_v,
    shared_left,
    shared_right,
    expert_m,
    expert_v,
    expert_left,
    expert_right,
    router_m,
    router_v,
    gains_m,
    gains_v,
):
    count, patches, width = images.shape
    hidden_width = up_weight.shape[2]
    experts = router_weight.shape[1]
    dp_size = lax.axis_size("dp")
    dp_index = lax.axis_index("dp")
    capacity = (42 * count * patches + 20 * experts - 1) // (20 * experts)
    places = round_up(capacity, 16)
    padded = round_up(patches, 16)
    tokens = count * padded
    router_pad = jnp.pad(router_weight, ((0, 0), (0, LANES - experts)))
    spare = ((0, 0), (0, padded - patches), (0, 0))
    choice = jnp.pad(choices, spare)
    slot = jnp.pad(slots, spare, constant_values=-1)
    choice_rows = choice.reshape(tokens, 2).T
    slot_rows = slot.reshape(tokens, 2).T

    qkv, attn, mixed, hidden, routed, probs, upstream = front(
        images, cotangent, gains, qkv_weight, out_weight, router_pad, experts, padded
    )
    outgoing, outgoing_grad = dispatch(
        choice_rows,
        slot_rows,
        routed.reshape(tokens, width),
        probs.reshape(tokens, LANES),
        upstream.reshape(tokens, width),
        experts,
        places,
    )

    def exchange(rows):
        return lax.all_to_all(rows, "expert", split_axis=0, concat_axis=0, tiled=True)

    total_places = experts * places
    arriving = exchange(outgoing).reshape(total_places, width)
    arriving_grad = exchange(outgoing_grad).reshape(total_places, width)
    act, slope, produced = ffn_fwd(arriving, up_weight, down_weight)
    returned = exchange(produced.reshape(experts, places, width))
    pre_grad, in_grad = ffn_bwd(arriving_grad, slope, up_weight, down_weight)
    returned_grad = exchange(in_grad.reshape(experts, places, width)).reshape(total_places, width)
    owner_row = owner_expert[0]
    expert_grads = expert_dw(owner_row, arriving, arriving_grad, act, pre_grad)
    expert_own = lax.psum_scatter(expert_grads, "dp", scatter_dimension=0, tiled=True)
    out, logit_low, router_grad = combine(
        choice, slot, returned, hidden, upstream, probs, routed, patches
    )
    grad_input, shared_grads, gain_grads = back(
        owner_shared, choice, slot, returned_grad, logit_low, router_pad, hidden, upstream, gains, out_weight,
        mixed, qkv, attn, qkv_weight, images, places,
    )
    shared_part = lax.psum_scatter(shared_grads, "dp", scatter_dimension=0, tiled=True)
    shared_own = lax.psum(shared_part, "expert")
    small = lax.psum(
        jnp.concatenate([router_grad[: round_up(experts, 8)], gain_grads], axis=0), ("dp", "expert")
    )
    router_total = small[:experts].T
    gains_total = small[round_up(experts, 8) : round_up(experts, 8) + 2]

    own_shared = owner_shared.shape[0] // dp_size
    own_expert = owner_row.shape[0] // dp_size
    my_shared = lax.dynamic_slice_in_dim(owner_shared, dp_index * own_shared, own_shared)
    my_expert = lax.dynamic_slice_in_dim(owner_row, dp_index * own_expert, own_expert)
    expert_m_new, expert_v_new, expert_w_new, expert_low = rotated_adam(
        my_expert, expert_own, up_weight[0], down_weight[0],
        expert_m[0], expert_v[0], expert_left[0], expert_right[0],
    )
    expert_all = lax.all_gather(expert_low, "dp", axis=0, tiled=True)
    shared_m_new, shared_v_new, shared_w_new, shared_low = rotated_adam(
        my_shared, shared_own, qkv_weight, out_weight, shared_m, shared_v, shared_left, shared_right
    )
    shared_all = lax.all_gather(shared_low, "dp", axis=0, tiled=True)
    router_m_new, router_v_new, router_w_new = plain_adam(
        router_total, router_weight.astype(f32), router_m, router_v, (0, 1)
    )
    gains_m_new, gains_v_new, gains_w_new = plain_adam(gains_total, gains, gains_m, gains_v, (1,))

    expert_slot = inverse(owner_row)
    shared_slot = inverse(owner_shared)
    up_count = (width // TILE) * (hidden_width // TILE)
    qkv_count = (width // TILE) * (3 * width // TILE)
    up_copy = untile(expert_slot[:up_count], expert_all, width, hidden_width)
    down_copy = untile(expert_slot[up_count:], expert_all, hidden_width, width)
    qkv_copy = untile(shared_slot[:qkv_count], shared_all, width, 3 * width)
    out_copy = untile(shared_slot[qkv_count:], shared_all, width, width)
    return (
        out,
        grad_input,
        shared_m_new,
        shared_v_new,
        shared_w_new,
        expert_m_new[None],
        expert_v_new[None],
        expert_w_new[None],
        router_m_new,
        router_v_new,
        router_w_new,
        gains_m_new,
        gains_v_new,
        gains_w_new,
        qkv_copy,
        out_copy,
        up_copy[None],
        down_copy[None],
    )


def solution(mesh):
    rows = P(("dp", "expert"), None, None)
    shared = P("dp", None, None)
    expert = P("expert", "dp", None, None)
    weight = P("expert", None, None)
    return jax.shard_map(
        shards,
        mesh=mesh,
        in_specs=(
            (rows, rows) + (P(),) * 4 + (weight, weight, rows, rows, P(), P("expert", None))
            + (shared,) * 4 + (expert,) * 4 + (P(),) * 4
        ),
        out_specs=(
            (rows, rows) + (shared,) * 3 + (expert,) * 3 + (P(),) * 8 + (weight, weight)
        ),
        check_vma=False,
    )
```

time: 1110 us -> 617 us (0.56)
  local copies, waits for them, and re-layouts: 415 us -> 20.4 us
  matrix products: 264 us -> 0 us
  Pallas kernels: 0 us -> 243 us
  other arithmetic: 157 us -> 2.26 us
  waiting for transfers between devices: 182 us -> 244 us
  blocking collectives: 45.8 us -> 78.2 us
    dot_general x29 -> x0, matrix products: 264 us -> none  [the longest x1 55.7 us: shards(): jnp.einsum('sjcd,jfd->sjcf', grouped_grad, down_weight, preferred_element...]
    pallas_call x0 -> x13, Pallas kernels: none -> 243 us  [the longest x1 47.8 us: back(): pl.pallas_call(functools.partial(back_body, patches=patches, places=place...]
    psum x1, waiting for transfers between devices: 182 us -> 1.11 us  [shards(): shared_own = lax.psum(shared_part, 'expert')]
    reduce_scatter x1 -> x2, waiting for transfers between devices: 0.01 us -> 149 us  [the longest x1 94.1 us: shards(): lax.psum_scatter(expert_grads, 'dp', scatter_dimension=0, tiled=True)]
    reshape x23 -> x2, local copies, waits for them, and re-layouts: 122 us -> 1.55 us  [the longest x1 0.78 us: shards(): slot_rows = slot.reshape(tokens, 2).T]
    gather x14 -> x0, local copies, waits for them, and re-layouts: 91 us -> none  [the longest x4 14.4 us: shards(): jnp.take_along_axis(router_probs, choice_rows, axis=1)]
    all_gather x2, waiting for transfers between devices: 0.01 us -> 69.1 us  [the longest x1 69.1 us: shards(): expert_all = lax.all_gather(expert_low, 'dp', axis=0, tiled=True)]
    transpose x8 -> x0, local copies, waits for them, and re-layouts: 48.2 us -> none  [the longest x4 23.7 us: to_tiles(): return jnp.swapaxes(blocked, -3, -2).reshape(leading + (-1, TILE, TILE))]
  transfers between devices with their start and end apart: 8 -> 8, of which waited for: 1 -> 6; matrix products, arithmetic and copies ran while one was open for 49% -> 2% of each run, Pallas kernels for 0% -> 24%
where the time goes in v1:
time: 617 us; the launch traced here: 615 us
  waiting for transfers between devices  244 us (40%)
  Pallas kernels  243 us (39%)
  blocking collectives  78.2 us (13%)
  local copies, waits for them, and re-layouts  20.4 us (3%)
  between operations  14.8 us (2%)
  starting transfers between devices  12.7 us (2%)
    reduce_scatter x1, waiting for transfers between devices, shards(): lax.psum_scatter(expert_grads, 'dp', scatter_dimension=0, tiled=True)  94.1 us
    all_gather x1, waiting for transfers between devices, shards(): expert_all = lax.all_gather(expert_low, 'dp', axis=0, tiled=True)  69.1 us
    reduce_scatter x1, waiting for transfers between devices, shards(): lax.psum_scatter(shared_grads, 'dp', scatter_dimension=0, tiled=True)  54.9 us
    pallas_call x1, Pallas kernels, back(): pl.pallas_call(functools.partial(back_body, patches=patches, places=place...  47.8 us
    pallas_call x1, Pallas kernels, expert_dw(): pl.pallas_call(functools.partial(expert_dw_body, up_cols=up_cols, down_co...  45.1 us
    psum x1, blocking collectives, shards(): lax.psum(jnp.concatenate([router_grad[:round_up(experts, 8)], gain_grads]...  41.6 us
    all_to_all x1, blocking collectives, exchange(): lax.all_to_all(rows, 'expert', split_axis=0, concat_axis=0, tiled=True)  36.5 us
    pallas_call x1, Pallas kernels, ffn_fwd(): pl.pallas_call(ffn_fwd_body, grid=(4,), in_specs=[row_blocks(block, width...  36 us
  transfers between devices with their start and end apart: 8, of which 6 were waited for; matrix products, arithmetic and copies ran while one was open for 2% of the time, Pallas kernels for 24%

profile of v1, /device:TPU:0, one launch (start us, length us, event | category | flops | bytes accessed | tf_op | source)
XLA Modules:
  0.0 615.0 jit_solution(13577931666532124963)
XLA Ops:
  7.2 1.0 copy.66
  8.2 0.9 copy.62
  11.6 1.2 copy.67.img
  12.8 2.4 copy.68.cot
  15.9 18.7 %front.1 = (bf16[4,208,2304]{2,1,0:T(8,128)(2,1)}, bf16[4,12,208,208]{3,2,1,0:T(8,128)(2,1)}, bf16[4,208,768]{2,1,0:T(8,128)(2,1)}, f32[4,208,768]{2,1,0:T(8,128...) custom-call(bf16[4,196,768]{2,1,0:T(8,128)(2,1)} %copy.67.img, ...), custom_call_target="tpu_custom_call" | custom-call | tf_op jit(solution)/shard_map/front/pallas_call | solution.py:130
  34.6 8.8 %dispatch.1 = (bf16[4,416,768]{2,1,0:T(8,128)(2,1)}, bf16[4,416,768]{2,1,0:T(8,128)(2,1)}) custom-call(s32[2,832]{1,0:T(2,128)} %bitcast.55, s32[2,832]{1,0:T(2,128)} %bitcast.56, bf16[832,768]{1,0:T(8,128)(2,1)} %bitcast.45, f32[832,128]{1,0:T(8,128)} %bitcast.54, bf16[832,768]{1,0:T(8,128)(2,1)} %bitcast.41), custom_call_target="tpu_custom_call" | custom-call | tf_op jit(solution)/shard_map/dispatch/pallas_call | solution.py:187
  43.4 36.5 %all_to_all.20 = bf16[4,416,768]{2,1,0:T(8,128)(2,1)} all-to-all(bf16[4,416,768]{2,1,0:T(8,128)(2,1)} %get-tuple-element.49), channel_id=1, replica_groups=mesh['dp'=8,'expert'=4] {'expert'}, dimensions={0} | all-to-all | bytes 5111808 | tf_op jit(solution)/shard_map/all_to_all | solution.py:670
  79.9 3.8 all-to-all-start.2
  83.7 36.0 %ffn_fwd.1 = (bf16[1664,3072]{1,0:T(8,128)(2,1)}, bf16[1664,3072]{1,0:T(8,128)(2,1)}, bf16[1664,768]{1,0:T(8,128)(2,1)}) custom-call(bf16[1664,768]{1,0:T(8,128)(2,1)} %bitcast.37, bf16[1,768,3072]{2,1,0:T(8,128)(2,1)} %up_w.3, bf16[1,3072,768]{2,1,0:T(8,128)(2,1)} %down_w.3), custom_call_target="tpu_custom_call" | custom-call | tf_op jit(solution)/shard_map/ffn_fwd/pallas_call | solution.py:235
  119.7 1.4 copy-done
  121.2 4.6 all-to-all-start.1
  125.7 24.4 %ffn_bwd.1 = (bf16[1664,3072]{1,0:T(8,128)(2,1)}, bf16[1664,768]{1,0:T(8,128)(2,1)}) custom-call(bf16[1664,768]{1,0:T(8,128)(2,1)} %bitcast.39, bf16[1664,3072]{1,0:T(8,128)(2,1)} %get-tuple-element.54.slope, bf16[1,768,3072]{2,1,0:T(8,128)(2,1)} %up_w.3, bf16[1,3072,768]{2,1,0:T(8,128)(2,1)} %down_w.3), custom_call_target="tpu_custom_call" | custom-call | tf_op jit(solution)/shard_map/ffn_bwd/pallas_call | solution.py:254
  150.2 4.9 all-to-all-done.1.returned
  155.1 3.6 all-to-all-start.3
  159.0 9.5 %combine.1 = (bf16[4,196,768]{2,1,0:T(8,128)(2,1)}, bf16[4,208,128]{2,1,0:T(8,128)(2,1)}, f32[128,768]{1,0:T(8,128)}) custom-call(s32[4,208,2]{2,1,0:T(8,128)} %copy-done.2, s32[4,208,2]{2,1,0:T(8,128)} %copy-done.3, bf16[4,416,768]{2,1,0:T(8,128)(2,1)} %all-to-all-done.1.returned, f32[4,208,768]{2,1,0:T(8,128)} %get-tuple-element.51.hidden, ...), custom_call_target="tpu_custom_call" | custom-call | tf_op jit(solution)/shard_map/combine/pallas_call | solution.py:354
  168.5 19.5 %all-to-all-done.3 = bf16[4,416,768]{2,1,0:T(8,128)(2,1)S(1)} async-done(((bf16[4,416,768]{2,1,0:T(8,128)(2,1)}), bf16[4,416,768]{2,1,0:T(8,128)(2,1)S(1)}, u32[]{:S(2)}, u32[]{:S(2)}) %all-to-all-start.3) | async-done | bytes 2555936 | tf_op jit(solution)/shard_map/all_to_all | solution.py:670
  188.0 1.5 copy-done.1
  189.5 47.8 %back.1 = (f32[4,196,768]{2,1,0:T(8,128)}, bf16[16,384,384]{2,1,0:T(8,128)(2,1)}, f32[8,768]{1,0:T(8,128)}) custom-call(s32[16]{0:T(128)} %owner.1, s32[4,208,2]{2,1,0:T(8,128)} %copy-done.2, s32[4,208,2]{2,1,0:T(8,128)} %copy-done.3, bf16[1664,768]{1,0:T(8,128)(2,1)} %bitcast.42, bf16[4,208,128]{2,1,0:T(8,128)(2,1)} %get-tuple-element.56.logit, ...), custom_call_target="tpu_custom_call" | custom-call | tf_op jit(solution)/shard_map/back/pallas_call | solution.py:479
  237.4 54.9 %reduce-scatter.3.cloned.1.call-done = bf16[2,384,384]{2,1,0:T(8,128)(2,1)} async-done(((bf16[16,384,384]{2,1,0:T(8,128)(2,1)}), bf16[2,384,384]{2,1,0:T(8,128)(2,1)}) %reduce-scatter.3.cloned.1.call-update) | async-done | bytes 589840 | tf_op jit(solution)/shard_map/reduce_scatter | solution.py:689
  292.4 45.1 %expert_dw.1 = bf16[32,384,384]{2,1,0:T(8,128)(2,1)} custom-call(s32[32]{0:T(128)} %bitcast.57, bf16[1664,768]{1,0:T(8,128)(2,1)} %bitcast.38, bf16[1664,768]{1,0:T(8,128)(2,1)} %bitcast.40, bf16[1664,3072]{1,0:T(8,128)(2,1)} %get-tuple-element.65.act, bf16[1664,3072]{1,0:T(8,128)(2,1)} %get-tuple-element.66.pre), custom_call_target="tpu_custom_call" | custom-call | tf_op jit(solution)/shard_map/expert_dw/pallas_call | solution.py:303
  338.7 1.1 all-reduce.5.cloned.1.call-done.grad
  339.8 6.8 %adam.2 = (f32[2,384,384]{2,1,0:T(8,128)}, f32[2,384,384]{2,1,0:T(8,128)}, f32[2,384,384]{2,1,0:T(8,128)}, bf16[2,384,384]{2,1,0:T(8,128)(2,1)}) custom-call(s32[2]{0:T(128)} %dynamic_slice.8.owner, bf16[2,384,384]{2,1,0:T(8,128)(2,1)} %all-reduce.5.cloned.1.call-done.grad, bf16[768,2304]{1,0:T(8,128)(2,1)} %w_one.1, bf16[768,768]{1,0:T(8,128)(2,1)} %w_two.1, ...), custom_call_target="tpu_custom_call" | custom-call | tf_op jit(solution)/shard_map/adam/pallas_call | solution.py:556
  347.6 94.1 %reduce-scatter.5.cloned.1.call-done.grad = bf16[4,384,384]{2,1,0:T(8,128)(2,1)} async-done(((bf16[32,384,384]{2,1,0:T(8,128)(2,1)}), bf16[4,384,384]{2,1,0:T(8,128)(2,1)}) %reduce-scatter.5.cloned.1.call-update) | async-done | bytes 1179664 | tf_op jit(solution)/shard_map/reduce_scatter | solution.py:681
  441.7 10.8 %adam.3 = (f32[4,384,384]{2,1,0:T(8,128)}, f32[4,384,384]{2,1,0:T(8,128)}, f32[4,384,384]{2,1,0:T(8,128)}, bf16[4,384,384]{2,1,0:T(8,128)(2,1)}) custom-call(s32[4]{0:T(128)} %dynamic-slice_bitcast_fusion.owner, bf16[4,384,384]{2,1,0:T(8,128)(2,1)} %reduce-scatter.5.cloned.1.call-done.grad, bf16[768,3072]{1,0:T(8,128)(2,1)} %bitcast.35, ...), custom_call_target="tpu_custom_call" | custom-call | tf_op jit(solution)/shard_map/adam/pallas_call | solution.py:556
  455.4 2.8 copy.70
  459.0 2.4 copy.71
  461.4 41.6 %psum.15 = f32[16,768]{1,0:T(8,128)S(1)} all-reduce(f32[16,768]{1,0:T(8,128)S(1)} %pad_maximum_fusion), channel_id=1, replica_groups=mesh['dp'=8,'expert'=4] {'dp','expert'}, use_global_device_ids=true, to_apply=%region_3.4 | all-reduce | flops 12288 | bytes 98304 | tf_op jit(solution)/shard_map/psum | solution.py:691
  504.3 4.2 untile.5
  508.5 8.8 %untile.4 = bf16[768,2304]{1,0:T(8,128)(2,1)} custom-call(s32[12]{0:T(128)} %bitcast.59, bf16[16,384,384]{2,1,0:T(8,128)(2,1)} %all-gather.3.cloned.1.call-done.tile), custom_call_target="tpu_custom_call" | custom-call | tf_op jit(solution)/shard_map/untile/pallas_call | solution.py:585
  517.3 69.1 %all-gather.5.cloned.1.call-done.tile = bf16[32,384,384]{2,1,0:T(8,128)(2,1)} async-done(((bf16[4,384,384]{2,1,0:T(8,128)(2,1)}), bf16[32,384,384]{2,1,0:T(8,128)(2,1)}) %all-gather.5.cloned.1.call-update) | async-done | bytes 9437200 | tf_op jit(solution)/shard_map/all_gather | solution.py:705
  586.3 11.1 %untile.7 = bf16[3072,768]{1,0:T(8,128)(2,1)} custom-call(s32[16]{0:T(128)} %get-tuple-element.134.slot_of, bf16[32,384,384]{2,1,0:T(8,128)(2,1)} %all-gather.5.cloned.1.call-done.tile), custom_call_target="tpu_custom_call" | custom-call | tf_op jit(solution)/shard_map/untile/pallas_call | solution.py:585
  597.4 11.1 %untile.6 = bf16[768,3072]{1,0:T(8,128)(2,1)} custom-call(s32[16]{0:T(128)} %get-tuple-element.135.slot_of, bf16[32,384,384]{2,1,0:T(8,128)(2,1)} %all-gather.5.cloned.1.call-done.tile), custom_call_target="tpu_custom_call" | custom-call | tf_op jit(solution)/shard_map/untile/pallas_call | solution.py:585
  (61 shorter events, 9.9 us)
Async XLA Ops:
  7.2 4.4 copy-start.5
  9.1 6.1 copy-start.2
  10.8 4.4 copy-start.3
  79.9 39.9 %all-to-all-start.2 = ((bf16[4,416,768]{2,1,0:T(8,128)(2,1)}), bf16[4,416,768]{2,1,0:T(8,128)(2,1)S(1)}, u32[]{:S(2)}, u32[]{:S(2)}) async-start(bf16[4,416,768]{2,1,0:T(8,128)(2,1)} %get-tuple-element.53), calls=%async_computation.2 | async-start | bytes 5111808 | tf_op jit(solution)/shard_map/all_to_all | solution.py:670
  119.7 1.4 copy-start
  121.2 33.9 %all-to-all-start.1 = ((bf16[4,416,768]{2,1,0:T(8,128)(2,1)}), bf16[4,416,768]{2,1,0:T(8,128)(2,1)}, u32[]{:S(2)}, u32[]{:S(2)}) async-start(bf16[4,416,768]{2,1,0:T(8,128)(2,1)} %bitcast.49), calls=%async_computation.1 | async-start | bytes 5111808 | tf_op jit(solution)/shard_map/all_to_all | solution.py:670
  155.1 32.9 %all-to-all-start.3 = ((bf16[4,416,768]{2,1,0:T(8,128)(2,1)}), bf16[4,416,768]{2,1,0:T(8,128)(2,1)S(1)}, u32[]{:S(2)}, u32[]{:S(2)}) async-start(bf16[4,416,768]{2,1,0:T(8,128)(2,1)} %bitcast.48), calls=%async_computation.3 | async-start | bytes 5111808 | tf_op jit(solution)/shard_map/all_to_all | solution.py:670
  158.8 133.6 %reduce-scatter.3.cloned.1.call-start = ((), (), s32[]{:S(2)}) async-start(), calls=%async_computation.6 | async-start | bytes 5308416 | tf_op jit(solution)/shard_map/reduce_scatter | solution.py:689
  188.0 1.5 copy-start.1
  237.3 102.5 %all-reduce.5.cloned.1.call-start = ((), (), s32[]{:S(2)}) async-start(), calls=%async_computation.7 | async-start | bytes 1179648 | tf_op jit(solution)/shard_map/psum | solution.py:690
  292.3 149.3 %reduce-scatter.5.cloned.1.call-start = ((), (), s32[]{:S(2)}) async-start(), calls=%async_computation.8 | async-start | bytes 10616832 | tf_op jit(solution)/shard_map/reduce_scatter | solution.py:681
  337.5 0.7 copy-start.13
  337.5 166.8 %all-gather.3.cloned.1.call-start = ((), (), s32[]{:S(2)}) async-start(), calls=%async_computation.9 | async-start | bytes 5308416 | tf_op jit(solution)/shard_map/all_gather | solution.py:709
  338.7 8.3 %copy-start.14 = (s32[1,32]{1,0:T(1,128)S(1)}, s32[1,32]{1,0:T(1,128)}, u32[]{:S(2)}) copy-start(s32[1,32]{1,0:T(1,128)} %param.35) | copy-start | bytes 388
  346.7 239.6 %all-gather.5.cloned.1.call-start = ((), (), s32[]{:S(2)}) async-start(), calls=%async_computation.10 | async-start | bytes 10616832 | tf_op jit(solution)/shard_map/all_gather | solution.py:705
  441.7 10.8 %copy-start.7 = (bf16[768,4]{0,1:T(4,128)(2,1)S(1)}, bf16[768,4]{0,1:T(4,128)(2,1)}, u32[]{:S(2)}) copy-start(bf16[768,4]{0,1:T(4,128)(2,1)} %param.29) | copy-start | bytes 18436
  441.7 13.0 %copy-start.6 = (f32[2,768]{1,0:T(2,128)S(1)}, f32[2,768]{1,0:T(2,128)}, u32[]{:S(2)}) copy-start(f32[2,768]{1,0:T(2,128)} %gains.3) | copy-start | bytes 18436
  452.5 6.5 %copy-start.4 = (f32[4,196,768]{2,1,0:T(8,128)S(1)}, f32[4,196,768]{2,1,0:T(8,128)}, u32[]{:S(2)}) copy-start(f32[4,196,768]{2,1,0:T(8,128)} %get-tuple-element.111) | copy-start | bytes 7225348
  454.0 7.3 %copy-start.15 = (s32[16]{0:T(128)}, s32[16]{0:T(128)S(1)}, u32[]{:S(2)}) copy-start(s32[16]{0:T(128)S(1)} %select_reduce_fusion.1) | copy-start | bytes 196
  459.0 2.4 copy-start.8
  459.0 44.0 %copy-start.11 = (f32[2,768]{1,0:T(2,128)S(1)}, f32[2,768]{1,0:T(2,128)}, u32[]{:S(2)}) copy-start(f32[2,768]{1,0:T(2,128)} %param.47) | copy-start | bytes 18436
  459.0 44.1 %copy-start.12 = (f32[2,768]{1,0:T(2,128)S(1)}, f32[2,768]{1,0:T(2,128)}, u32[]{:S(2)}) copy-start(f32[2,768]{1,0:T(2,128)} %param.46) | copy-start | bytes 18436
  459.0 44.7 %copy-start.9 = (f32[768,4]{0,1:T(4,128)S(1)}, f32[768,4]{0,1:T(4,128)}, u32[]{:S(2)}) copy-start(f32[768,4]{0,1:T(4,128)} %param.45) | copy-start | bytes 36868
  459.0 44.7 %copy-start.10 = (f32[768,4]{0,1:T(4,128)S(1)}, f32[768,4]{0,1:T(4,128)}, u32[]{:S(2)}) copy-start(f32[768,4]{0,1:T(4,128)} %param.44) | copy-start | bytes 36868
Sparse Core Ops, SparseCore 0:
  237.4 54.8 reduce-scatter.2
  295.3 44.4 all-reduce.4
  342.1 99.4 reduce-scatter.4
  443.7 50.6 all-gather.2
  496.5 89.7 all-gather.4

commit v2 on v1

--- a/solution.py
+++ b/solution.py
@@ -6,6 +6,7 @@
 from jax.experimental import pallas as pl
 from jax.experimental.pallas import tpu as pltpu
 from jax.sharding import PartitionSpec as P
+
 
 HEADS = 12
 HEAD_DIM = 64
@@ -270,56 +271,65 @@
     )(g, slope, up_w, down_w)
 
 
-def expert_dw_body(owner, x, g, act, pre, tile_o, *, up_cols, down_cols, up_count):
-    tile = owner[pl.program_id(0)]
-
-    @pl.when(tile < up_count)
+def turn(rows):
+    width = rows.shape[1]
+    same = lax.broadcasted_iota(jnp.int32, (width, width), 0) == lax.broadcasted_iota(
+        jnp.int32, (width, width), 1
+    )
+    return dot_nt(jnp.where(same, 1.0, 0.0).astype(bf16), rows).astype(bf16)
+
+
+DW_CHUNK = 2 * TILE
+
+
+def expert_dw_body(slot_of, x, g, act, pre, after, tile_o, x_turned, g_turned, *, up_cols, down_cols):
+    step = pl.program_id(0)
+
+    @pl.when(step == 0)
     def _():
-        row = pl.multiple_of(tile // up_cols * TILE, TILE)
-        tile_o[0] = dot_tn(x[:, pl.ds(row, TILE)], pre[...]).astype(bf16)
-
-    @pl.when(tile >= up_count)
-    def _():
-        col = pl.multiple_of((tile - up_count) % down_cols * TILE, TILE)
-        tile_o[0] = dot_tn(act[...], g[:, pl.ds(col, TILE)]).astype(bf16)
-
-
-def expert_dw(owner, x, g, act, pre):
+        x_turned[...] = turn(x[...])
+        g_turned[...] = turn(g[...])
+
+    up_count = up_cols * down_cols
+    part = dot_nn(x_turned[...], pre[...]).astype(bf16)
+    for row in range(down_cols):
+        for col in range(2):
+            slot = slot_of[row * up_cols + 2 * step + col]
+            tile_o[slot] = part[row * TILE : (row + 1) * TILE, col * TILE : (col + 1) * TILE]
+    part = dot_nn(g_turned[...], act[...]).astype(bf16)
+    for row in range(2):
+        for col in range(down_cols):
+            slot = slot_of[up_count + (2 * step + row) * down_cols + col]
+            tile_o[slot] = part[col * TILE : (col + 1) * TILE, row * TILE : (row + 1) * TILE].T
+
+
+def expert_dw(slot_of, x, g, act, pre, after):
     rows, width = x.shape
     hidden = act.shape[1]
-    up_cols = hidden // TILE
-    down_cols = width // TILE
-    up_count = up_cols * down_cols
-    count = owner.shape[0]
-
-    def pre_at(i, owner):
-        tile = owner[i]
-        return (0, jnp.where(tile < up_count, tile % up_cols, 0))
-
-    def act_at(i, owner):
-        tile = owner[i]
-        return (0, jnp.where(tile >= up_count, (tile - up_count) // down_cols, 0))
-
+    count = slot_of.shape[0]
+    columns = pl.BlockSpec((rows, DW_CHUNK), lambda i, slot_of: (0, i))
     return pl.pallas_call(
-        functools.partial(expert_dw_body, up_cols=up_cols, down_cols=down_cols, up_count=up_count),
+        functools.partial(expert_dw_body, up_cols=hidden // TILE, down_cols=width // TILE),
         grid_spec=pltpu.PrefetchScalarGridSpec(
             num_scalar_prefetch=1,
-            grid=(count,),
+            grid=(hidden // DW_CHUNK,),
             in_specs=[
                 full((rows, width)),
                 full((rows, width)),
-                pl.BlockSpec((rows, TILE), act_at),
-                pl.BlockSpec((rows, TILE), pre_at),
+                columns,
+                columns,
+                pl.BlockSpec(memory_space=pl.ANY),
             ],
-            out_specs=per((TILE, TILE)),
+            out_specs=full((count, TILE, TILE)),
+            scratch_shapes=[pltpu.VMEM((width, rows), bf16), pltpu.VMEM((width, rows), bf16)],
         ),
         out_shape=jax.ShapeDtypeStruct((count, TILE, TILE), bf16),
         compiler_params=params(),
         name="expert_dw",
-    )(owner, x, g, act, pre)
-
-
-def combine_body(choice, slot, returned, hidden, upstream, probs, routed, out_o, logit_o, router_o, *, patches):
+    )(slot_of, x, g, act, pre, after)
+
+
+def combine_body(choice, slot, returned, hidden, upstream, probs, routed, after, later, out_o, logit_o, router_o, *, patches):
     experts, places = returned.shape[0], returned.shape[1]
     up = upstream[0].astype(f32)
     prob = probs[0]
@@ -349,7 +359,7 @@
     router_o[...] += dot_tn(logit, routed[0])
 
 
-def combine(choice, slot, returned, hidden, upstream, probs, routed, patches):
+def combine(choice, slot, returned, hidden, upstream, probs, routed, patches, after, later):
     count, padded, width = hidden.shape
     return pl.pallas_call(
         functools.partial(combine_body, patches=patches),
@@ -362,6 +372,8 @@
             per((padded, width)),
             per((padded, LANES)),
             per((padded, width)),
+            pl.BlockSpec(memory_space=pl.ANY),
+            pl.BlockSpec(memory_space=pl.ANY),
         ],
         out_specs=[per((patches, width)), per((padded, LANES)), full((LANES, width))],
         out_shape=[
@@ -371,13 +383,14 @@
         ],
         compiler_params=params(),
         name="combine",
-    )(choice, slot, returned, hidden, upstream, probs, routed)
+    )(choice, slot, returned, hidden, upstream, probs, routed, after, later)
 
 
 def back_body(
     owner, choice, slot, returned, logit, router_w, hidden, upstream, gains, out_w, mixed, qkv, attn, qkv_w, img,
     grad_o, tile_o, gain_o,
     rows, normed_all, qkv_grad_all, mixed_all, branch_all, mixed_grad_s, hidden_grad_s,
+    normed_turned, mixed_turned,
     *, patches, places
 ):
     image = pl.program_id(0)
@@ -442,6 +455,8 @@
 
     @pl.when(image == pl.num_programs(0) - 1)
     def _():
+        normed_turned[...] = turn(normed_all[...])
+        mixed_turned[...] = turn(mixed_all[...])
         row_tiles = width // TILE
         qkv_cols = 3 * row_tiles
         qkv_count = row_tiles * qkv_cols
@@ -453,8 +468,8 @@
             def _():
                 row = pl.multiple_of(tile // qkv_cols * TILE, TILE)
                 col = pl.multiple_of(tile % qkv_cols * TILE, TILE)
-                tile_o[s] = dot_tn(
-                    normed_all[:, pl.ds(row, TILE)], qkv_grad_all[:, pl.ds(col, TILE)]
+                tile_o[s] = dot_nn(
+                    normed_turned[pl.ds(row, TILE), :], qkv_grad_all[:, pl.ds(col, TILE)]
                 ).astype(bf16)
 
             @pl.when(tile >= qkv_count)
@@ -462,8 +477,8 @@
                 rest = tile - qkv_count
                 row = pl.multiple_of(rest // row_tiles * TILE, TILE)
                 col = pl.multiple_of(rest % row_tiles * TILE, TILE)
-                tile_o[s] = dot_tn(
-                    mixed_all[:, pl.ds(row, TILE)], branch_all[:, pl.ds(col, TILE)]
+                tile_o[s] = dot_nn(
+                    mixed_turned[pl.ds(row, TILE), :], branch_all[:, pl.ds(col, TILE)]
                 ).astype(bf16)
 
             return carry
@@ -506,6 +521,8 @@
                 pltpu.VMEM((count * padded, width), bf16),
                 pltpu.VMEM((padded, width), bf16),
                 pltpu.VMEM((padded, width), f32),
+                pltpu.VMEM((width, count * padded), bf16),
+                pltpu.VMEM((width, count * padded), bf16),
             ],
         ),
         out_shape=[
@@ -575,30 +592,80 @@
     )(owner, grad, w_one, w_two, m, v, left, right)
 
 
-def untile_body(slot_of, tile, out):
-    out[...] = tile[0]
-
-
-def untile(slot_of, tiles, row_count, col_count):
-    cols = col_count // TILE
-    count = slot_of.shape[0]
+def untile_body(slot_of, *refs):
+    outs = refs[-2:]
+    tiles = refs[:-2]
+    for out in outs:
+        cols = out.shape[1] // TILE
+        count = out.shape[0] // TILE * cols
+        for index in range(count):
+            row, col = index // cols * TILE, index % cols * TILE
+            out[row : row + TILE, col : col + TILE] = tiles[index][0]
+        tiles = tiles[count:]
+
+
+def untile(slot_of, tiles, one_shape, two_shape, one_blocks, two_blocks):
+    steps = one_blocks
+    specs = []
+    one_rows, one_cols = one_shape[0] // TILE, one_shape[1] // TILE
+    two_rows, two_cols = two_shape[0] // TILE, two_shape[1] // TILE
+    wide = one_cols // steps
+    high = two_rows // two_blocks
+    for row in range(one_rows):
+        for col in range(wide):
+            specs.append(
+                pl.BlockSpec(
+                    (1, TILE, TILE),
+                    lambda i, slot_of, row=row, col=col: (slot_of[row * one_cols + i * wide + col], 0, 0),
+                )
+            )
+    base = one_rows * one_cols
+    for row in range(high):
+        for col in range(two_cols):
+            specs.append(
+                pl.BlockSpec(
+                    (1, TILE, TILE),
+                    lambda i, slot_of, row=row, col=col: (
+                        slot_of[base + (jnp.minimum(i, two_blocks - 1) * high + row) * two_cols + col], 0, 0,
+                    ),
+                )
+            )
     return pl.pallas_call(
         untile_body,
         grid_spec=pltpu.PrefetchScalarGridSpec(
             num_scalar_prefetch=1,
-            grid=(count,),
-            in_specs=[pl.BlockSpec((1, TILE, TILE), lambda i, slot_of: (slot_of[i], 0, 0))],
-            out_specs=pl.BlockSpec((TILE, TILE), lambda i, slot_of: (i // cols, i % cols)),
+            grid=(steps,),
+            in_specs=specs,
+            out_specs=[
+                pl.BlockSpec((one_shape[0], wide * TILE), lambda i, slot_of: (0, i)),
+                pl.BlockSpec(
+                    (high * TILE, two_shape[1]),
+                    lambda i, slot_of: (jnp.minimum(i, two_blocks - 1), 0),
+                ),
+            ],
         ),
-        out_shape=jax.ShapeDtypeStruct((row_count, col_count), bf16),
+        out_shape=[jax.ShapeDtypeStruct(one_shape, bf16), jax.ShapeDtypeStruct(two_shape, bf16)],
         compiler_params=params(),
         name="untile",
-    )(slot_of, tiles)
+    )(slot_of, *([tiles] * len(specs)))
 
 
 def inverse(owner):
     ids = jnp.arange(owner.shape[0], dtype=jnp.int32)
     return jnp.sum(jnp.where(owner[None, :] == ids[:, None], ids[None, :], 0), axis=1)
+
+
+def sum_over_expert(rows):
+    size = lax.axis_size("expert")
+    bits = [1 << b for b in range(size.bit_length() - 1)]
+    half = rows.shape[1] // 2
+    parts = [rows[:, :half], rows[:, half:]]
+    for step in range(len(bits)):
+        for which in range(2):
+            bit = bits[step] if which == 0 else bits[-1 - step]
+            other = lax.ppermute(parts[which], "expert", [(i, i ^ bit) for i in range(size)])
+            parts[which] = (parts[which].astype(f32) + other.astype(f32)).astype(bf16)
+    return jnp.concatenate(parts, axis=1)
 
 
 def plain_adam(grad_values, weight_values, first_moment, second_moment, axes):
@@ -611,7 +678,7 @@
     return (first_new, second_new, weight_values - step_rate * direction)
 
 
-def shards(
+def step(
     images,
     cotangent,
     gains,
@@ -677,17 +744,20 @@
     pre_grad, in_grad = ffn_bwd(arriving_grad, slope, up_weight, down_weight)
     returned_grad = exchange(in_grad.reshape(experts, places, width)).reshape(total_places, width)
     owner_row = owner_expert[0]
-    expert_grads = expert_dw(owner_row, arriving, arriving_grad, act, pre_grad)
+    expert_slot = inverse(owner_row)
+    shared_slot = inverse(owner_shared)
+    expert_grads = expert_dw(expert_slot, arriving, arriving_grad, act, pre_grad, returned)
     expert_own = lax.psum_scatter(expert_grads, "dp", scatter_dimension=0, tiled=True)
     out, logit_low, router_grad = combine(
-        choice, slot, returned, hidden, upstream, probs, routed, patches
+        choice, slot, returned, hidden, upstream, probs, routed, patches, expert_grads, expert_grads
     )
     grad_input, shared_grads, gain_grads = back(
         owner_shared, choice, slot, returned_grad, logit_low, router_pad, hidden, upstream, gains, out_weight,
         mixed, qkv, attn, qkv_weight, images, places,
     )
+    shared_grads, expert_own = lax.optimization_barrier((shared_grads, expert_own))
     shared_part = lax.psum_scatter(shared_grads, "dp", scatter_dimension=0, tiled=True)
-    shared_own = lax.psum(shared_part, "expert")
+    shared_own = sum_over_expert(shared_part)
     small = lax.psum(
         jnp.concatenate([router_grad[: round_up(experts, 8)], gain_grads], axis=0), ("dp", "expert")
     )
@@ -712,14 +782,10 @@
     )
     gains_m_new, gains_v_new, gains_w_new = plain_adam(gains_total, gains, gains_m, gains_v, (1,))
 
-    expert_slot = inverse(owner_row)
-    shared_slot = inverse(owner_shared)
-    up_count = (width // TILE) * (hidden_width // TILE)
-    qkv_count = (width // TILE) * (3 * width // TILE)
-    up_copy = untile(expert_slot[:up_count], expert_all, width, hidden_width)
-    down_copy = untile(expert_slot[up_count:], expert_all, hidden_width, width)
-    qkv_copy = untile(shared_slot[:qkv_count], shared_all, width, 3 * width)
-    out_copy = untile(shared_slot[qkv_count:], shared_all, width, width)
+    up_copy, down_copy = untile(
+        expert_slot, expert_all, (width, hidden_width), (hidden_width, width), 4, 4
+    )
+    qkv_copy, out_copy = untile(shared_slot, shared_all, (width, 3 * width), (width, width), 3, 2)
     return (
         out,
         grad_input,
@@ -748,7 +814,7 @@
     expert = P("expert", "dp", None, None)
     weight = P("expert", None, None)
     return jax.shard_map(
-        shards,
+        step,
         mesh=mesh,
         in_specs=(
             (rows, rows) + (P(),) * 4 + (weight, weight, rows, rows, P(), P("expert", None))

time: 617 us -> 503 us (0.82)
  waiting for transfers between devices: 244 us -> 146 us
  Pallas kernels: 243 us -> 210 us
  blocking collectives: 78.2 us -> 84.5 us
    reduce_scatter x2, waiting for transfers between devices: 149 us -> 60.4 us  [the longest x1 44.5 us: step(): lax.psum_scatter(shared_grads, 'dp', scatter_dimension=0, tiled=True)]
    pallas_call x4 -> x2, Pallas kernels: 35.1 us -> 14.2 us  [untile(): pl.pallas_call(untile_body, grid_spec=pltpu.PrefetchScalarGridSpec(num_sc...]
    all_gather x2, waiting for transfers between devices: 69.1 us -> 52.9 us  [the longest x1 43.5 us: step(): shared_all = lax.all_gather(shared_low, 'dp', axis=0, tiled=True)]
    pallas_call x1, Pallas kernels: 45.1 us -> 31.2 us  [expert_dw(): pl.pallas_call(functools.partial(expert_dw_body, up_cols=hidden // TILE,...]
    ppermute x0 -> x4, waiting for transfers between devices: none -> 10.8 us  [sum_over_expert(): lax.ppermute(parts[which], 'expert', [(i, i ^ bit) for i in range(size)])]
    psum x1, blocking collectives: 41.6 us -> 47.9 us  [step(): lax.psum(jnp.concatenate([router_grad[:round_up(experts, 8)], gain_grads]...]
    unnamed x39 -> x45, local copies, waits for them, and re-layouts: 15.1 us -> 12.6 us
  transfers between devices with their start and end apart: 8 -> 11, of which waited for: 6 -> 10; matrix products, arithmetic and copies ran while one was open for 2% -> 3% of each run, Pallas kernels for 24% -> 29%
where the time goes in v2:
time: 503 us; the launch traced here: 498 us
  Pallas kernels  210 us (42%)
  waiting for transfers between devices  146 us (29%)
  blocking collectives  84.5 us (17%)
  local copies, waits for them, and re-layouts  18 us (4%)
  starting transfers between devices  18 us (4%)
  between operations  14.9 us (3%)
  other arithmetic  5.67 us (1%)
    pallas_call x1, Pallas kernels, back(): pl.pallas_call(functools.partial(back_body, patches=patches, places=place...  49.3 us
    psum x1, blocking collectives, step(): lax.psum(jnp.concatenate([router_grad[:round_up(experts, 8)], gain_grads]...  47.9 us
    reduce_scatter x1, waiting for transfers between devices, step(): lax.psum_scatter(shared_grads, 'dp', scatter_dimension=0, tiled=True)  44.5 us
    all_gather x1, waiting for transfers between devices, step(): shared_all = lax.all_gather(shared_low, 'dp', axis=0, tiled=True)  43.5 us
    all_to_all x1, blocking collectives, exchange(): lax.all_to_all(rows, 'expert', split_axis=0, concat_axis=0, tiled=True)  36.6 us
    pallas_call x1, Pallas kernels, ffn_fwd(): pl.pallas_call(ffn_fwd_body, grid=(4,), in_specs=[row_blocks(block, width...  36 us
    pallas_call x1, Pallas kernels, expert_dw(): pl.pallas_call(functools.partial(expert_dw_body, up_cols=hidden // TILE,...  31.2 us
    pallas_call x1, Pallas kernels, ffn_bwd(): pl.pallas_call(ffn_bwd_body, grid=(4,), in_specs=[row_blocks(block, width...  24.6 us
  transfers between devices with their start and end apart: 11, of which 10 were waited for; matrix products, arithmetic and copies ran while one was open for 3% of the time, Pallas kernels for 29%

profile of v2, /device:TPU:0, one launch (start us, length us, event | category | flops | bytes accessed | tf_op | source)
XLA Modules:
  0.0 497.6 jit_solution(480580145937847943)
XLA Ops:
  7.2 2.5 copy.67.img
  13.9 18.7 %front.1 = (bf16[4,208,2304]{2,1,0:T(8,128)(2,1)}, bf16[4,12,208,208]{3,2,1,0:T(8,128)(2,1)}, bf16[4,208,768]{2,1,0:T(8,128)(2,1)}, f32[4,208,768]{2,1,0:T(8,128...) custom-call(bf16[4,196,768]{2,1,0:T(8,128)(2,1)} %copy.67.img, ...), custom_call_target="tpu_custom_call" | custom-call | tf_op jit(solution)/shard_map/front/pallas_call | solution.py:131
  32.5 8.8 %dispatch.1 = (bf16[4,416,768]{2,1,0:T(8,128)(2,1)}, bf16[4,416,768]{2,1,0:T(8,128)(2,1)}) custom-call(s32[2,832]{1,0:T(2,128)} %bitcast.52, s32[2,832]{1,0:T(2,128)} %bitcast.53, bf16[832,768]{1,0:T(8,128)(2,1)} %bitcast.44, f32[832,128]{1,0:T(8,128)} %bitcast.51, bf16[832,768]{1,0:T(8,128)(2,1)} %bitcast.40), custom_call_target="tpu_custom_call" | custom-call | tf_op jit(solution)/shard_map/dispatch/pallas_call | solution.py:188
  41.3 36.6 %all_to_all.20 = bf16[4,416,768]{2,1,0:T(8,128)(2,1)} all-to-all(bf16[4,416,768]{2,1,0:T(8,128)(2,1)} %get-tuple-element.55), channel_id=1, replica_groups=mesh['dp'=8,'expert'=4] {'expert'}, dimensions={0} | all-to-all | bytes 5111808 | tf_op jit(solution)/shard_map/all_to_all | solution.py:737
  77.9 3.9 all-to-all-start.2
  81.8 36.0 %ffn_fwd.1 = (bf16[1664,3072]{1,0:T(8,128)(2,1)}, bf16[1664,3072]{1,0:T(8,128)(2,1)}, bf16[1664,768]{1,0:T(8,128)(2,1)}) custom-call(bf16[1664,768]{1,0:T(8,128)(2,1)} %bitcast.36, bf16[1,768,3072]{2,1,0:T(8,128)(2,1)} %up_w.3, bf16[1,3072,768]{2,1,0:T(8,128)(2,1)} %down_w.3), custom_call_target="tpu_custom_call" | custom-call | tf_op jit(solution)/shard_map/ffn_fwd/pallas_call | solution.py:236
  117.9 1.5 copy-done.1
  119.3 4.2 all-to-all-start.1
  124.7 24.6 %ffn_bwd.1 = (bf16[1664,3072]{1,0:T(8,128)(2,1)}, bf16[1664,768]{1,0:T(8,128)(2,1)}) custom-call(bf16[1664,768]{1,0:T(8,128)(2,1)} %bitcast.38, bf16[1664,3072]{1,0:T(8,128)(2,1)} %get-tuple-element.60.slope, bf16[1,768,3072]{2,1,0:T(8,128)(2,1)} %up_w.3, bf16[1,3072,768]{2,1,0:T(8,128)(2,1)} %down_w.3), custom_call_target="tpu_custom_call" | custom-call | tf_op jit(solution)/shard_map/ffn_bwd/pallas_call | solution.py:255
  149.3 3.0 all-to-all-done.1.after.returned
  153.7 31.2 %expert_dw.1.after.later = bf16[32,384,384]{2,1,0:T(8,128)(2,1)} custom-call(s32[32]{0:T(128)} %select_reduce_fusion.slot_of, bf16[1664,768]{1,0:T(8,128)(2,1)} %bitcast.37, bf16[1664,768]{1,0:T(8,128)(2,1)} %bitcast.39, bf16[1664,3072]{1,0:T(8,128)(2,1)} %get-tuple-element.59.act, bf16[1664,3072]{1,0:T(8,128)(2,1)} %get-tuple-element.61.pre, ...), custom_call_target="tpu_custom_call" | custom-call | tf_op jit(solution)/shard_map/expert_dw/pallas_call | solution.py:311
  185.0 3.7 all-to-all-start.3
  188.9 9.8 %combine.1 = (bf16[4,196,768]{2,1,0:T(8,128)(2,1)}, bf16[4,208,128]{2,1,0:T(8,128)(2,1)}, f32[128,768]{1,0:T(8,128)}) custom-call(s32[4,208,2]{2,1,0:T(8,128)} %copy-done.3, s32[4,208,2]{2,1,0:T(8,128)} %copy-done.4, bf16[4,416,768]{2,1,0:T(8,128)(2,1)} %copy-done, f32[4,208,768]{2,1,0:T(8,128)} %get-tuple-element.57.hidden, ...), custom_call_target="tpu_custom_call" | custom-call | tf_op jit(solution)/shard_map/combine/pallas_call | solution.py:364
  198.6 19.3 %all-to-all-done.3 = bf16[4,416,768]{2,1,0:T(8,128)(2,1)S(1)} async-done(((bf16[4,416,768]{2,1,0:T(8,128)(2,1)}), bf16[4,416,768]{2,1,0:T(8,128)(2,1)S(1)}, u32[]{:S(2)}, u32[]{:S(2)}) %all-to-all-start.3) | async-done | bytes 2555936 | tf_op jit(solution)/shard_map/all_to_all | solution.py:737
  217.9 1.5 copy-done.2
  219.4 49.3 %back.1 = (f32[4,196,768]{2,1,0:T(8,128)}, bf16[16,384,384]{2,1,0:T(8,128)(2,1)}, f32[8,768]{1,0:T(8,128)}) custom-call(s32[16]{0:T(128)} %owner.1, s32[4,208,2]{2,1,0:T(8,128)} %copy-done.3, s32[4,208,2]{2,1,0:T(8,128)} %copy-done.4, bf16[1664,768]{1,0:T(8,128)(2,1)} %bitcast.41, bf16[4,208,128]{2,1,0:T(8,128)(2,1)} %get-tuple-element.64.logit, ...), custom_call_target="tpu_custom_call" | custom-call | tf_op jit(solution)/shard_map/back/pallas_call | solution.py:494
  268.7 15.9 %reduce-scatter.3.cloned.1.call-done.grad = bf16[4,384,384]{2,1,0:T(8,128)(2,1)} async-done(((bf16[32,384,384]{2,1,0:T(8,128)(2,1)}), bf16[4,384,384]{2,1,0:T(8,128)(2,1)}) %reduce-scatter.3.cloned.1.call-update) | async-done | bytes 1179664 | tf_op jit(solution)/shard_map/reduce_scatter | solution.py:750
  285.2 10.7 %adam.3 = (f32[4,384,384]{2,1,0:T(8,128)}, f32[4,384,384]{2,1,0:T(8,128)}, f32[4,384,384]{2,1,0:T(8,128)}, bf16[4,384,384]{2,1,0:T(8,128)(2,1)}) custom-call(s32[4]{0:T(128)} %dynamic-slice_bitcast_fusion.owner, bf16[4,384,384]{2,1,0:T(8,128)(2,1)} %reduce-scatter.3.cloned.1.call-done.grad, bf16[768,3072]{1,0:T(8,128)(2,1)} %bitcast.34, ...), custom_call_target="tpu_custom_call" | custom-call | tf_op jit(solution)/shard_map/adam/pallas_call | solution.py:573
  296.2 44.5 %reduce-scatter.5.cloned.1.call-done = bf16[2,384,384]{2,1,0:T(8,128)(2,1)} async-done(((bf16[16,384,384]{2,1,0:T(8,128)(2,1)}), bf16[2,384,384]{2,1,0:T(8,128)(2,1)}) %reduce-scatter.5.cloned.1.call-update) | async-done | bytes 589840 | tf_op jit(solution)/shard_map/reduce_scatter | solution.py:759
  341.9 1.5 collective-permute-start
  343.4 1.5 collective-permute-start.2
  344.9 3.9 collective-permute-done
  351.4 1.6 collective-permute-start.1
  354.1 4.0 collective-permute-done.1
  358.2 1.5 collective-permute-done.3
  360.7 7.1 %adam.2 = (f32[2,384,384]{2,1,0:T(8,128)}, f32[2,384,384]{2,1,0:T(8,128)}, f32[2,384,384]{2,1,0:T(8,128)}, bf16[2,384,384]{2,1,0:T(8,128)(2,1)}) custom-call(s32[2]{0:T(128)} %dynamic_slice.8.owner, bf16[2,384,384]{2,1,0:T(8,128)(2,1)} %pad_maximum_fusion.grad, bf16[768,2304]{1,0:T(8,128)(2,1)} %w_one.1, bf16[768,768]{1,0:T(8,128)(2,1)} %w_two.1, ...), custom_call_target="tpu_custom_call" | custom-call | tf_op jit(solution)/shard_map/adam/pallas_call | solution.py:573
  370.6 2.4 copy.71
  374.5 47.9 %psum.7 = f32[16,768]{1,0:T(8,128)S(1)} all-reduce(f32[16,768]{1,0:T(8,128)S(1)} %pad_maximum_fusion.1), channel_id=1, replica_groups=mesh['dp'=8,'expert'=4] {'dp','expert'}, use_global_device_ids=true, to_apply=%region_3.4 | all-reduce | flops 12288 | bytes 98304 | tf_op jit(solution)/shard_map/psum | solution.py:761
  423.8 9.4 %all-gather.5.cloned.1.call-done.refs_0_.refs_1_.refs_2_.refs_3_.refs_4_.refs_5_.refs_6_.refs_7_ = bf16[32,384,384]{2,1,0:T(8,128)(2,1)} async-done(((bf16[4,384,384]{2,1,0:T(8,128)(2,1)}), bf16[32,384,384]{2,1,0:T(8,128)(2,1)}) %all-gather.5.cloned.1.call-update) | async-done | bytes 9437200 | tf_op jit(solution)/shard_map/all_gather | solution.py:775
  433.2 8.3 %untile.3 = (bf16[768,3072]{1,0:T(8,128)(2,1)}, bf16[3072,768]{1,0:T(8,128)(2,1)}) custom-call(s32[32]{0:T(128)} %select_reduce_fusion.slot_of, bf16[32,384,384]{2,1,0:T(8,128)(2,1)} %all-gather.5.cloned.1.call-done.refs_0_.refs_1_.refs_2_.refs_3_.refs_4_.refs_5_.refs_6_.refs_7_, ...), custom_call_target="tpu_custom_call" | custom-call | tf_op jit(solution)/shard_map/untile/pallas_call | solution.py:633
  441.5 43.5 %all-gather.3.cloned.1.call-done.refs_0_.refs_1_.refs_2_.refs_3_.refs_4_.refs_5_ = bf16[16,384,384]{2,1,0:T(8,128)(2,1)} async-done(((bf16[2,384,384]{2,1,0:T(8,128)(2,1)}), bf16[16,384,384]{2,1,0:T(8,128)(2,1)}) %all-gather.3.cloned.1.call-update) | async-done | bytes 4718608 | tf_op jit(solution)/shard_map/all_gather | solution.py:779
  484.9 5.9 %untile.2 = (bf16[768,2304]{1,0:T(8,128)(2,1)}, bf16[768,768]{1,0:T(8,128)(2,1)}) custom-call(s32[16]{0:T(128)} %select_reduce_fusion.1.slot_of, bf16[16,384,384]{2,1,0:T(8,128)(2,1)} %all-gather.3.cloned.1.call-done.refs_0_.refs_1_.refs_2_.refs_3_.refs_4_.refs_5_, ...), custom_call_target="tpu_custom_call" | custom-call | tf_op jit(solution)/shard_map/untile/pallas_call | solution.py:633
  (73 shorter events, 18.7 us)
Async XLA Ops:
  7.2 2.6 copy-start.9
  7.2 2.7 copy-start.7
  7.2 3.9 copy-start.13
  9.8 2.4 copy-start.14
  11.3 21.2 %copy-start.3 = (s32[4,208,2]{2,1,0:T(8,128)}, s32[4,208,2]{2,1,0:T(8,128)S(1)}, u32[]{:S(2)}) copy-start(s32[4,208,2]{2,1,0:T(8,128)S(1)} %pad.11.choice) | copy-start | bytes 19972
  12.4 20.2 %copy-start.4 = (s32[4,208,2]{2,1,0:T(8,128)}, s32[4,208,2]{2,1,0:T(8,128)S(1)}, u32[]{:S(2)}) copy-start(s32[4,208,2]{2,1,0:T(8,128)S(1)} %pad.12.slot) | copy-start | bytes 19972
  77.9 40.0 %all-to-all-start.2 = ((bf16[4,416,768]{2,1,0:T(8,128)(2,1)}), bf16[4,416,768]{2,1,0:T(8,128)(2,1)S(1)}, u32[]{:S(2)}, u32[]{:S(2)}) async-start(bf16[4,416,768]{2,1,0:T(8,128)(2,1)} %get-tuple-element.58), calls=%async_computation.2 | async-start | bytes 5111808 | tf_op jit(solution)/shard_map/all_to_all | solution.py:737
  117.8 1.5 copy-start.1
  117.8 6.2 %copy-start.18 = (s32[1,32]{1,0:T(1,128)S(1)}, s32[1,32]{1,0:T(1,128)}, u32[]{:S(2)}) copy-start(s32[1,32]{1,0:T(1,128)} %param.35) | copy-start | bytes 388
  119.3 32.9 %all-to-all-start.1 = ((bf16[4,416,768]{2,1,0:T(8,128)(2,1)}), bf16[4,416,768]{2,1,0:T(8,128)(2,1)S(1)}, u32[]{:S(2)}, u32[]{:S(2)}) async-start(bf16[4,416,768]{2,1,0:T(8,128)(2,1)} %bitcast.46), calls=%async_computation.1 | async-start | bytes 5111808 | tf_op jit(solution)/shard_map/all_to_all | solution.py:737
  123.5 161.0 %reduce-scatter.3.cloned.1.call-start = ((), (), s32[]{:S(2)}) async-start(), calls=%async_computation.6 | async-start | bytes 10616832 | tf_op jit(solution)/shard_map/reduce_scatter | solution.py:750
  152.3 1.5 copy-start
  185.0 32.9 %all-to-all-start.3 = ((bf16[4,416,768]{2,1,0:T(8,128)(2,1)}), bf16[4,416,768]{2,1,0:T(8,128)(2,1)S(1)}, u32[]{:S(2)}, u32[]{:S(2)}) async-start(bf16[4,416,768]{2,1,0:T(8,128)(2,1)} %bitcast.45), calls=%async_computation.3 | async-start | bytes 5111808 | tf_op jit(solution)/shard_map/all_to_all | solution.py:737
  188.6 152.1 %reduce-scatter.5.cloned.1.call-start = ((), (), s32[]{:S(2)}) async-start(), calls=%async_computation.7 | async-start | bytes 5308416 | tf_op jit(solution)/shard_map/reduce_scatter | solution.py:759
  217.9 1.5 copy-start.2
  284.6 148.6 %all-gather.5.cloned.1.call-start = ((), (), s32[]{:S(2)}) async-start(), calls=%async_computation.9 | async-start | bytes 10616832 | tf_op jit(solution)/shard_map/all_gather | solution.py:775
  295.9 57.6 %copy-start.17 = (s32[16]{0:T(128)S(1)}, s32[16]{0:T(128)}, u32[]{:S(2)}) copy-start(s32[16]{0:T(128)} %owner.1) | copy-start | bytes 196
  296.0 189.0 %all-gather.3.cloned.1.call-start = ((), (), s32[]{:S(2)}) async-start(), calls=%async_computation.8 | async-start | bytes 5308416 | tf_op jit(solution)/shard_map/all_gather | solution.py:779
  341.9 6.9 %collective-permute-start = (bf16[2,192,384]{2,1,0:T(8,128)(2,1)S(1)}, bf16[2,192,384]{2,1,0:T(8,128)(2,1)S(1)}, u32[]{:S(2)}, u32[]{:S(2)}) collective-permute-start(bf16[2,192,384]{2,1,0:T(8,128)(2,1)S(1)} %get-tuple-element.148), channel_id=1, source_target_pairs={{0,1},{1,0},{2,3},{3,2},{4,5},{5,4},{6,7},{7,6},{8,9},{9,8},{10,11... | collective-permute-start | bytes 884744 | tf_op jit(solution)/shard_map/ppermute | solution.py:666
  343.4 6.7 %collective-permute-start.2 = (bf16[2,192,384]{2,1,0:T(8,128)(2,1)S(1)}, bf16[2,192,384]{2,1,0:T(8,128)(2,1)S(1)}, u32[]{:S(2)}, u32[]{:S(2)}) collective-permute-start(bf16[2,192,384]{2,1,0:T(8,128)(2,1)S(1)} %get-tuple-element.149), channel_id=1, source_target_pairs={{0,2},{1,3},{2,0},{3,1},{4,6},{5,7},{6,4},{7,5},{8,10},{9,11},{10,... | collective-permute-start | bytes 884744 | tf_op jit(solution)/shard_map/ppermute | solution.py:666
  351.4 6.8 %collective-permute-start.1 = (bf16[2,192,384]{2,1,0:T(8,128)(2,1)S(1)}, bf16[2,192,384]{2,1,0:T(8,128)(2,1)S(1)}, u32[]{:S(2)}, u32[]{:S(2)}) collective-permute-start(bf16[2,192,384]{2,1,0:T(8,128)(2,1)S(1)} %get-tuple-element.146), channel_id=1, source_target_pairs={{0,2},{1,3},{2,0},{3,1},{4,6},{5,7},{6,4},{7,5},{8,10},{9,11},{10,... | collective-permute-start | bytes 884744 | tf_op jit(solution)/shard_map/ppermute | solution.py:666
  353.0 6.7 %collective-permute-start.3 = (bf16[2,192,384]{2,1,0:T(8,128)(2,1)S(1)}, bf16[2,192,384]{2,1,0:T(8,128)(2,1)S(1)}, u32[]{:S(2)}, u32[]{:S(2)}) collective-permute-start(bf16[2,192,384]{2,1,0:T(8,128)(2,1)S(1)} %get-tuple-element.147), channel_id=1, source_target_pairs={{0,1},{1,0},{2,3},{3,2},{4,5},{5,4},{6,7},{7,6},{8,9},{9,8},{10,11... | collective-permute-start | bytes 884744 | tf_op jit(solution)/shard_map/ppermute | solution.py:666
  360.7 9.1 %copy-start.8 = (f32[2,768]{1,0:T(2,128)S(1)}, f32[2,768]{1,0:T(2,128)}, u32[]{:S(2)}) copy-start(f32[2,768]{1,0:T(2,128)} %gains.3) | copy-start | bytes 18436
  360.7 10.0 %copy-start.5 = (f32[4,196,768]{2,1,0:T(8,128)S(1)}, f32[4,196,768]{2,1,0:T(8,128)}, u32[]{:S(2)}) copy-start(f32[4,196,768]{2,1,0:T(8,128)} %get-tuple-element.123) | copy-start | bytes 7225348
  370.6 2.4 copy-start.6
  373.0 1.5 copy-start.10
  373.0 49.5 %copy-start.15 = (f32[2,768]{1,0:T(2,128)S(1)}, f32[2,768]{1,0:T(2,128)}, u32[]{:S(2)}) copy-start(f32[2,768]{1,0:T(2,128)} %param.47) | copy-start | bytes 18436
  373.0 49.5 %copy-start.16 = (f32[2,768]{1,0:T(2,128)S(1)}, f32[2,768]{1,0:T(2,128)}, u32[]{:S(2)}) copy-start(f32[2,768]{1,0:T(2,128)} %param.46) | copy-start | bytes 18436
  373.0 50.1 %copy-start.11 = (f32[768,4]{0,1:T(4,128)S(1)}, f32[768,4]{0,1:T(4,128)}, u32[]{:S(2)}) copy-start(f32[768,4]{0,1:T(4,128)} %param.45) | copy-start | bytes 36868
  373.0 50.1 %copy-start.12 = (f32[768,4]{0,1:T(4,128)S(1)}, f32[768,4]{0,1:T(4,128)}, u32[]{:S(2)}) copy-start(f32[768,4]{0,1:T(4,128)} %param.44) | copy-start | bytes 36868
Sparse Core Ops, SparseCore 0:
  185.1 99.3 reduce-scatter.2
  287.4 53.3 reduce-scatter.4
  343.0 90.1 all-gather.4
  435.2 49.6 all-gather.2
